TPU v7x, 256 devices: a whole 4x4x8 slice. The times are simulated.
256 devices in a mesh: river: 8 (over y, core), leaf: 32 (over z, x).
Axes of the slice: x: 4, y: 4, z: 8, core: 2. Of those that a mesh axis runs over, the one named last changes fastest.
Arguments:
- range_zero: float32 [16, 1344], P(None, 'leaf'), may hold values from 0.0001 to 0.001
- range_one: float32 [16, 1344], P(None, 'leaf'), may hold values from 0.0001 to 0.001
- turn_regret: float32 [8, 16, 1344], P('river', None, 'leaf'), may hold values from 0.05 to 5
- river_regret_zero: float32 [8, 1344, 3072], P('river', 'leaf'), may hold values from 0.05 to 5
- river_regret_one: float32 [8, 1344, 9216], P('river', 'leaf'), may hold values from 0.05 to 5
- hand_cards: int32 [1344, 2], replicated, may hold values from 0 to 52, as said below
- dealt_cards: int32 [52], replicated, may hold values from 0 to 51, as said below
- hand_ranks: int32 [48, 1344], replicated, may hold values from 0 to 7461
- leaf_pots: int32 [8, 12], P('river'), may hold values from 2 to 64
- leaf_kinds: int32 [8, 12], P('river'), may hold values from 0 to 2
Outputs:
- new_turn_regret: float32 [8, 16, 1344], P('river', None, 'leaf')
- new_river_zero: float32 [8, 1344, 3072], P('river', 'leaf')
- new_river_one: float32 [8, 1344, 9216], P('river', 'leaf')
- root_values: float32 [2, 16, 1344], P(None, None, 'leaf')
Inputs may be any that keep to these rules, and one draw needn't show every extreme that they name: `hand_cards`: each slot holds the two card numbers of a distinct two-card hand; every one of the 1,326 hands has a slot; empty slots hold 52 twice. `dealt_cards`: all entries are distinct card numbers. `hand_ranks`: A higher rank wins the showdown, equal ranks split it. `leaf_kinds`: 0 is a showdown, 1 a fold by player one, 2 a fold by player zero.
All inputs are finite; a program needn't handle non-finite values.
Results may differ from a plain program's by a relative error of at most 0.0003.
Values may be sent and summed in bfloat16 or wider, within the bound.
A program may use at most 128 MiB of HBM per device.

v0:
```python
import jax
import jax.numpy as jnp
from jax import lax
from jax.sharding import PartitionSpec as P

MOVES_ZERO = 4
MOVES_ONE = 3


chance_weight = 1.0 / 44.0


def hand_validity(hand_cards, dealt_cards):
    first_card = hand_cards[:, 0]
    second_card = hand_cards[:, 1]
    board_cards = dealt_cards[:4]
    river_cards = dealt_cards[4:]
    on_board = jnp.any(first_card[:, None] == board_cards[None, :], axis=1) | jnp.any(
        second_card[:, None] == board_cards[None, :], axis=1
    )
    usable = (first_card < 52) & (second_card < 52) & jnp.logical_not(on_board)
    blocked = (first_card[None, :] == river_cards[:, None]) | (
        second_card[None, :] == river_cards[:, None]
    )
    return (usable[None, :] & jnp.logical_not(blocked)).astype(jnp.float32)


def card_intersection(hand_cards):
    first_card = hand_cards[:, 0]
    second_card = hand_cards[:, 1]
    shared = (first_card[:, None] == first_card[None, :]) | (
        first_card[:, None] == second_card[None, :]
    )
    shared = (
        shared
        | (second_card[:, None] == first_card[None, :])
        | (second_card[:, None] == second_card[None, :])
    )
    return jnp.logical_not(shared).astype(jnp.float32)


def payoff_block(validity, disjoint, ranking, pot_value, kind_value):
    showdown = jnp.sign(ranking[:, None] - ranking[None, :]).astype(jnp.float32)
    outcome = jnp.where(kind_value == 0, showdown, jnp.where(kind_value == 1, 1.0, -1.0))
    scaled = (
        pot_value.astype(jnp.float32) * outcome * disjoint * validity[:, None] * validity[None, :]
    )
    return scaled.astype(jnp.bfloat16)


def local(
    range_zero,
    range_one,
    turn_regret,
    river_regret_zero,
    river_regret_one,
    hand_cards,
    dealt_cards,
    hand_ranks,
    leaf_pots,
    leaf_kinds,
):
    line_count = turn_regret.shape[0]
    subgames = range_zero.shape[0]
    hand_shard = range_zero.shape[1]
    rivers = hand_ranks.shape[0]
    moves_zero = MOVES_ZERO
    moves_one = MOVES_ONE
    leaves = moves_zero * moves_one
    per_device = rivers * leaves // lax.axis_size("leaf")
    group_count = per_device // moves_one
    regret_zero = river_regret_zero.reshape(line_count, hand_shard, rivers, moves_zero, subgames)
    regret_one = river_regret_one.reshape(
        line_count, hand_shard, rivers, moves_zero, moves_one, subgames
    )
    zero_share = regret_zero / jnp.sum(regret_zero, axis=3, keepdims=True)
    one_share = regret_one / jnp.sum(regret_one, axis=4, keepdims=True)
    opponent = jnp.transpose(range_one)
    one_reach = (opponent[None, :, None, None, None, :] * one_share).astype(jnp.bfloat16)
    one_reach = jnp.transpose(
        one_reach.reshape(line_count, hand_shard, rivers * leaves, subgames), (0, 2, 3, 1)
    )
    turn_total = lax.psum(jnp.sum(turn_regret, axis=0), "river")
    turn_share = turn_regret / turn_total[None]
    weighted = jnp.swapaxes(range_zero[None] * turn_share, 1, 2)
    reach_rounded = (weighted[:, :, None, None, :] * zero_share).astype(jnp.bfloat16)
    zero_groups = lax.all_to_all(
        jnp.transpose(
            reach_rounded.reshape(line_count, hand_shard, rivers * moves_zero, subgames),
            (0, 2, 3, 1),
        ),
        "leaf",
        split_axis=1,
        concat_axis=3,
        tiled=True,
    )
    one_blocks = lax.all_to_all(one_reach, "leaf", split_axis=1, concat_axis=3, tiled=True)
    validity = hand_validity(hand_cards, dealt_cards)
    disjoint = card_intersection(hand_cards)
    group_first = lax.axis_index("leaf") * per_device + moves_one * jnp.arange(
        group_count, dtype=jnp.int32
    )
    river_ids = group_first // leaves
    leaf_ids = (group_first % leaves)[:, None] + jnp.arange(moves_one, dtype=jnp.int32)[None, :]
    group_pots = leaf_pots[:, leaf_ids]
    group_kinds = leaf_kinds[:, leaf_ids]
    all_hands = zero_groups.shape[3]

    def group_values(group_items):
        zero_group, one_group, river_index, pot_values, kind_values = group_items
        payoffs = jax.vmap(payoff_block, in_axes=(None, None, None, 0, 0))(
            validity[river_index], disjoint, hand_ranks[river_index], pot_values, kind_values
        )
        zero_value = lax.dot_general(
            one_group, payoffs, (((2,), (2,)), ((0,), (0,))), preferred_element_type=jnp.float32
        )
        one_value = -lax.dot_general(
            zero_group, payoffs, (((1,), (1,)), ((), ())), preferred_element_type=jnp.float32
        )
        return (zero_value, jnp.swapaxes(one_value, 0, 1))

    total_groups = line_count * group_count
    zero_values, one_values = lax.map(
        group_values,
        (
            zero_groups.reshape(total_groups, subgames, all_hands),
            one_blocks.reshape(total_groups, moves_one, subgames, all_hands),
            jnp.tile(river_ids, line_count),
            group_pots.reshape(total_groups, moves_one),
            group_kinds.reshape(total_groups, moves_one),
        ),
    )
    zero_values = zero_values.reshape(line_count, group_count, moves_one, subgames, all_hands)
    one_values = one_values.reshape(line_count, per_device, subgames, all_hands)
    zero_back, one_back = (
        lax.all_to_all(
            zero_values.reshape(line_count, per_device, subgames, all_hands),
            "leaf",
            split_axis=3,
            concat_axis=1,
            tiled=True,
        ),
        lax.all_to_all(one_values, "leaf", split_axis=3, concat_axis=1, tiled=True),
    )
    summed = jnp.sum(
        zero_back.reshape(line_count, rivers, moves_zero, moves_one, subgames, hand_shard), axis=3
    )
    action_zero = jnp.transpose(summed, (0, 4, 1, 2, 3))
    leaf_one = jnp.transpose(
        one_back.reshape(line_count, rivers, moves_zero, moves_one, subgames, hand_shard),
        (0, 5, 1, 2, 3, 4),
    )
    node_zero = jnp.sum(zero_share * action_zero, axis=3)
    new_zero = jnp.maximum(regret_zero + action_zero - node_zero[:, :, :, None, :], 0.0)
    node_one = jnp.sum(one_share * leaf_one, axis=4)
    new_one = jnp.maximum(regret_one + leaf_one - node_one[:, :, :, :, None, :], 0.0)
    line_zero = jnp.swapaxes(chance_weight * jnp.sum(node_zero, axis=2), 1, 2)
    line_one = jnp.swapaxes(chance_weight * jnp.sum(node_one, axis=(2, 3)), 1, 2)
    root_zero, root_one = lax.psum(
        (jnp.sum(turn_share * line_zero, axis=0), jnp.sum(line_one, axis=0)), "river"
    )
    new_turn = jnp.maximum(turn_regret + line_zero - root_zero[None], 0.0)
    new_zero_out = new_zero.reshape(line_count, hand_shard, -1)
    new_one_out = new_one.reshape(line_count, hand_shard, -1)
    return (new_turn, new_zero_out, new_one_out, jnp.stack([root_zero, root_one]))


def solution(mesh):
    placed = (
        P(None, "leaf"),
        P(None, "leaf"),
        P("river", None, "leaf"),
        P("river", "leaf", None),
        P("river", "leaf", None),
        P(),
        P(),
        P(),
        P("river", None),
        P("river", None),
    )
    return jax.shard_map(
        local,
        mesh=mesh,
        in_specs=placed,
        out_specs=(
            P("river", None, "leaf"),
            P("river", "leaf", None),
            P("river", "leaf", None),
            P(None, None, "leaf"),
        ),
        check_vma=False,
    )
```

profile of v0, /device:TPU:38, one launch (start us, length us, event | category | flops | bytes accessed | tf_op | source)
XLA Modules:
  0.0 473.1 jit_solution(1104247043423840625)
XLA Ops:
  0.6 1.5 copy.81
  2.2 15.2 %psum.21 = f32[1,16,42]{2,1,0:T(8,128)S(1)} all-reduce(f32[1,16,42]{2,1,0:T(8,128)} %param.14), channel_id=1, replica_groups=mesh['river'=8,'leaf'=32] {'river'}, use_global_device_ids=true, to_apply=%region_1.0 | all-reduce | flops 672 | bytes 5376 | tf_op jit(solution)/shard_map/psum | solution.py:83
  17.7 1.4 fusion.21
  19.2 2.1 reshape.324
  21.3 11.1 %all-to-all-start.1 = ((bf16[32,2,2016]{2,1,0:T(2,128)(2,1)}), bf16[32,2,2016]{2,1,0:T(2,128)(2,1)S(1)}, u32[]{:S(2)}, u32[]{:S(2)}) async-start(bf16[32,2,2016]{2,1,0:T(2,128)(2,1)} %reshape.324), calls=%async_computation.1 | async-start | bytes 524288 | tf_op jit(solution)/shard_map/all_to_all | solution.py:87
  32.4 5.8 %copy.82 = f32[1,42,9216]{1,2,0:T(8,128)} copy(f32[1,42,9216]{2,0,1:T(1,128)} %param.16) | data formatting | bytes 3096576 | tf_op args[4]
  38.2 3.2 reduce_sum.84
  42.6 1.7 copy-done.4
  44.4 2.1 fusion.27
  46.5 5.5 %reshape.322 = bf16[32,2,6048]{2,1,0:T(2,128)(2,1)} reshape(bf16[576,1,16,42]{3,2,1,0:T(8,128)(2,1)} %fusion.27) | data formatting | bytes 1548288
  52.0 10.2 %all-to-all-start = ((bf16[32,2,6048]{2,1,0:T(2,128)(2,1)}), bf16[32,2,6048]{2,1,0:T(2,128)(2,1)S(1)}, u32[]{:S(2)}, u32[]{:S(2)}) async-start(bf16[32,2,6048]{2,1,0:T(2,128)(2,1)} %reshape.322), calls=%async_computation | async-start | bytes 1572864 | tf_op jit(solution)/shard_map/all_to_all | solution.py:97
  64.4 1.4 reshape.325
  66.1 2.1 reshape.282
  68.3 12.6 %all-to-all-done = bf16[32,2,6048]{2,1,0:T(2,128)(2,1)S(1)} async-done(((bf16[32,2,6048]{2,1,0:T(2,128)(2,1)}), bf16[32,2,6048]{2,1,0:T(2,128)(2,1)S(1)}, u32[]{:S(2)}, u32[]{:S(2)}) %all-to-all-start) | async-done | bytes 774176 | tf_op jit(solution)/shard_map/all_to_all | solution.py:97
  80.9 4.2 reshape.323
  85.1 2.4 copy.85
  87.5 4.7 %reshape.278 = bf16[6,3,16,1344]{3,2,1,0:T(8,128)(2,1)S(1)} reshape(bf16[1,18,16,32,42]{4,3,2,1,0:T(8,128)(2,1)} %copy.85) | data formatting | bytes 1548288 | tf_op jit(solution)/shard_map/reshape | solution.py:127
  92.3 177.7 %while.13 = (s32[]{:T(128)}, f32[6,3,16,1344]{3,2,1,0:T(8,128)}, f32[6,3,16,1344]{3,2,1,0:T(8,128)}, bf16[6,3,16,1344]{3,2,1,0:T(8,128)(2,1)S(1)}, s32[6,3]{1,0:...) while((s32[]{:T(128)}, f32[6,3,16,1344]{3,2,1,0:T(8,128)}, ...), condition=%wide.region_6.7_spmd.clone, body=%wide.region_5.0_spmd.clone.sunk | while | flops 433585152 | bytes 74426408 | solution.py:123
  96.0 1.5 sign_convert_fusion.2
  97.7 5.3 %not_convert_fusion.2 = f32[1344,1344]{1,0:T(8,128)} fusion(s32[1344]{0:T(1024)S(1)} %get-tuple-element.268, s32[1344]{0:T(1024)S(1)} %get-tuple-element.267), kind=kLoop, calls=%fused_computation.5.clone.1 | loop fusion | flops 16257024 | bytes 7236096 | tf_op jit(solution)/shard_map/convert_element_type | solution.py:39
  103.0 8.8 %fusion.39 = f32[6,3,16,1344]{3,2,1,0:T(8,128)} fusion(f32[6,3,16,1344]{3,2,1,0:T(8,128)} %get-tuple-element.244, s32[]{:T(128)} %get-tuple-element.242, f32[1344]{0:T(1024)S(1)} %dynamic-slice_reduce_fusion.4, f32[1344,1344]{1,0:T(8,128)} %not_convert_fusion.2, f32[3]{0:T(128)S(1)} %fusion.36, f32[1344,1344]{1,0:T(8,128)S(1)} %sign_convert_fusion.2, ...), kind=kOutput, calls=%fused_computation.8.clone.1 | convolution fusion | flops 205986816 | bytes 15473152 | tf_op jit(solution)/shard_map/while/body/eval_jaxpr/dot_general | solution.py:117
  111.8 10.3 %fusion.38 = f32[6,3,16,1344]{3,2,1,0:T(8,128)} fusion(f32[6,3,16,1344]{3,2,1,0:T(8,128)} %get-tuple-element.243, s32[]{:T(128)} %get-tuple-element.242, bf16[6,3,16,1344]{3,2,1,0:T(8,128)(2,1)S(1)} %get-tuple-element.260, f32[1344]{0:T(1024)S(1)} %dynamic-slice_reduce_fusion.4, f32[1344,1344]{1,0:T(8,128)} %not_convert_fusion.2, f32[3]{0:T(128)S(1)} %fusion.36, ...), kind=kOutput, calls=%fused_computation.10.clone.1 | convolution fusion | flops 205922304 | bytes 15563264 | tf_op jit(solution)/shard_map/while/body/eval_jaxpr/dot_general | solution.py:114
  125.5 1.5 sign_convert_fusion.2
  127.2 5.3 %not_convert_fusion.2 = f32[1344,1344]{1,0:T(8,128)} fusion(s32[1344]{0:T(1024)S(1)} %get-tuple-element.268, s32[1344]{0:T(1024)S(1)} %get-tuple-element.267), kind=kLoop, calls=%fused_computation.5.clone.1 | loop fusion | flops 16257024 | bytes 7236096 | tf_op jit(solution)/shard_map/convert_element_type | solution.py:39
  132.5 8.9 %fusion.39 = f32[6,3,16,1344]{3,2,1,0:T(8,128)} fusion(f32[6,3,16,1344]{3,2,1,0:T(8,128)} %get-tuple-element.244, s32[]{:T(128)} %get-tuple-element.242, f32[1344]{0:T(1024)S(1)} %dynamic-slice_reduce_fusion.4, f32[1344,1344]{1,0:T(8,128)} %not_convert_fusion.2, f32[3]{0:T(128)S(1)} %fusion.36, f32[1344,1344]{1,0:T(8,128)S(1)} %sign_convert_fusion.2, ...), kind=kOutput, calls=%fused_computation.8.clone.1 | convolution fusion | flops 205986816 | bytes 15473152 | tf_op jit(solution)/shard_map/while/body/eval_jaxpr/dot_general | solution.py:117
  141.4 10.3 %fusion.38 = f32[6,3,16,1344]{3,2,1,0:T(8,128)} fusion(f32[6,3,16,1344]{3,2,1,0:T(8,128)} %get-tuple-element.243, s32[]{:T(128)} %get-tuple-element.242, bf16[6,3,16,1344]{3,2,1,0:T(8,128)(2,1)S(1)} %get-tuple-element.260, f32[1344]{0:T(1024)S(1)} %dynamic-slice_reduce_fusion.4, f32[1344,1344]{1,0:T(8,128)} %not_convert_fusion.2, f32[3]{0:T(128)S(1)} %fusion.36, ...), kind=kOutput, calls=%fused_computation.10.clone.1 | convolution fusion | flops 205922304 | bytes 15563264 | tf_op jit(solution)/shard_map/while/body/eval_jaxpr/dot_general | solution.py:114
  155.0 1.5 sign_convert_fusion.2
  156.7 5.3 %not_convert_fusion.2 = f32[1344,1344]{1,0:T(8,128)} fusion(s32[1344]{0:T(1024)S(1)} %get-tuple-element.268, s32[1344]{0:T(1024)S(1)} %get-tuple-element.267), kind=kLoop, calls=%fused_computation.5.clone.1 | loop fusion | flops 16257024 | bytes 7236096 | tf_op jit(solution)/shard_map/convert_element_type | solution.py:39
  162.0 8.9 %fusion.39 = f32[6,3,16,1344]{3,2,1,0:T(8,128)} fusion(f32[6,3,16,1344]{3,2,1,0:T(8,128)} %get-tuple-element.244, s32[]{:T(128)} %get-tuple-element.242, f32[1344]{0:T(1024)S(1)} %dynamic-slice_reduce_fusion.4, f32[1344,1344]{1,0:T(8,128)} %not_convert_fusion.2, f32[3]{0:T(128)S(1)} %fusion.36, f32[1344,1344]{1,0:T(8,128)S(1)} %sign_convert_fusion.2, ...), kind=kOutput, calls=%fused_computation.8.clone.1 | convolution fusion | flops 205986816 | bytes 15473152 | tf_op jit(solution)/shard_map/while/body/eval_jaxpr/dot_general | solution.py:117
  170.9 10.3 %fusion.38 = f32[6,3,16,1344]{3,2,1,0:T(8,128)} fusion(f32[6,3,16,1344]{3,2,1,0:T(8,128)} %get-tuple-element.243, s32[]{:T(128)} %get-tuple-element.242, bf16[6,3,16,1344]{3,2,1,0:T(8,128)(2,1)S(1)} %get-tuple-element.260, f32[1344]{0:T(1024)S(1)} %dynamic-slice_reduce_fusion.4, f32[1344,1344]{1,0:T(8,128)} %not_convert_fusion.2, f32[3]{0:T(128)S(1)} %fusion.36, ...), kind=kOutput, calls=%fused_computation.10.clone.1 | convolution fusion | flops 205922304 | bytes 15563264 | tf_op jit(solution)/shard_map/while/body/eval_jaxpr/dot_general | solution.py:114
  184.6 1.5 sign_convert_fusion.2
  186.2 5.3 %not_convert_fusion.2 = f32[1344,1344]{1,0:T(8,128)} fusion(s32[1344]{0:T(1024)S(1)} %get-tuple-element.268, s32[1344]{0:T(1024)S(1)} %get-tuple-element.267), kind=kLoop, calls=%fused_computation.5.clone.1 | loop fusion | flops 16257024 | bytes 7236096 | tf_op jit(solution)/shard_map/convert_element_type | solution.py:39
  191.6 8.8 %fusion.39 = f32[6,3,16,1344]{3,2,1,0:T(8,128)} fusion(f32[6,3,16,1344]{3,2,1,0:T(8,128)} %get-tuple-element.244, s32[]{:T(128)} %get-tuple-element.242, f32[1344]{0:T(1024)S(1)} %dynamic-slice_reduce_fusion.4, f32[1344,1344]{1,0:T(8,128)} %not_convert_fusion.2, f32[3]{0:T(128)S(1)} %fusion.36, f32[1344,1344]{1,0:T(8,128)S(1)} %sign_convert_fusion.2, ...), kind=kOutput, calls=%fused_computation.8.clone.1 | convolution fusion | flops 205986816 | bytes 15473152 | tf_op jit(solution)/shard_map/while/body/eval_jaxpr/dot_general | solution.py:117
  200.4 10.3 %fusion.38 = f32[6,3,16,1344]{3,2,1,0:T(8,128)} fusion(f32[6,3,16,1344]{3,2,1,0:T(8,128)} %get-tuple-element.243, s32[]{:T(128)} %get-tuple-element.242, bf16[6,3,16,1344]{3,2,1,0:T(8,128)(2,1)S(1)} %get-tuple-element.260, f32[1344]{0:T(1024)S(1)} %dynamic-slice_reduce_fusion.4, f32[1344,1344]{1,0:T(8,128)} %not_convert_fusion.2, f32[3]{0:T(128)S(1)} %fusion.36, ...), kind=kOutput, calls=%fused_computation.10.clone.1 | convolution fusion | flops 205922304 | bytes 15563264 | tf_op jit(solution)/shard_map/while/body/eval_jaxpr/dot_general | solution.py:114
  214.1 1.5 sign_convert_fusion.2
  215.7 5.3 %not_convert_fusion.2 = f32[1344,1344]{1,0:T(8,128)} fusion(s32[1344]{0:T(1024)S(1)} %get-tuple-element.268, s32[1344]{0:T(1024)S(1)} %get-tuple-element.267), kind=kLoop, calls=%fused_computation.5.clone.1 | loop fusion | flops 16257024 | bytes 7236096 | tf_op jit(solution)/shard_map/convert_element_type | solution.py:39
  221.1 8.8 %fusion.39 = f32[6,3,16,1344]{3,2,1,0:T(8,128)} fusion(f32[6,3,16,1344]{3,2,1,0:T(8,128)} %get-tuple-element.244, s32[]{:T(128)} %get-tuple-element.242, f32[1344]{0:T(1024)S(1)} %dynamic-slice_reduce_fusion.4, f32[1344,1344]{1,0:T(8,128)} %not_convert_fusion.2, f32[3]{0:T(128)S(1)} %fusion.36, f32[1344,1344]{1,0:T(8,128)S(1)} %sign_convert_fusion.2, ...), kind=kOutput, calls=%fused_computation.8.clone.1 | convolution fusion | flops 205986816 | bytes 15473152 | tf_op jit(solution)/shard_map/while/body/eval_jaxpr/dot_general | solution.py:117
  229.9 10.3 %fusion.38 = f32[6,3,16,1344]{3,2,1,0:T(8,128)} fusion(f32[6,3,16,1344]{3,2,1,0:T(8,128)} %get-tuple-element.243, s32[]{:T(128)} %get-tuple-element.242, bf16[6,3,16,1344]{3,2,1,0:T(8,128)(2,1)S(1)} %get-tuple-element.260, f32[1344]{0:T(1024)S(1)} %dynamic-slice_reduce_fusion.4, f32[1344,1344]{1,0:T(8,128)} %not_convert_fusion.2, f32[3]{0:T(128)S(1)} %fusion.36, ...), kind=kOutput, calls=%fused_computation.10.clone.1 | convolution fusion | flops 205922304 | bytes 15563264 | tf_op jit(solution)/shard_map/while/body/eval_jaxpr/dot_general | solution.py:114
  243.6 1.5 sign_convert_fusion.2
  245.2 5.3 %not_convert_fusion.2 = f32[1344,1344]{1,0:T(8,128)} fusion(s32[1344]{0:T(1024)S(1)} %get-tuple-element.268, s32[1344]{0:T(1024)S(1)} %get-tuple-element.267), kind=kLoop, calls=%fused_computation.5.clone.1 | loop fusion | flops 16257024 | bytes 7236096 | tf_op jit(solution)/shard_map/convert_element_type | solution.py:39
  250.6 8.9 %fusion.39 = f32[6,3,16,1344]{3,2,1,0:T(8,128)} fusion(f32[6,3,16,1344]{3,2,1,0:T(8,128)} %get-tuple-element.244, s32[]{:T(128)} %get-tuple-element.242, f32[1344]{0:T(1024)S(1)} %dynamic-slice_reduce_fusion.4, f32[1344,1344]{1,0:T(8,128)} %not_convert_fusion.2, f32[3]{0:T(128)S(1)} %fusion.36, f32[1344,1344]{1,0:T(8,128)S(1)} %sign_convert_fusion.2, ...), kind=kOutput, calls=%fused_computation.8.clone.1 | convolution fusion | flops 205986816 | bytes 15473152 | tf_op jit(solution)/shard_map/while/body/eval_jaxpr/dot_general | solution.py:117
  259.4 10.3 %fusion.38 = f32[6,3,16,1344]{3,2,1,0:T(8,128)} fusion(f32[6,3,16,1344]{3,2,1,0:T(8,128)} %get-tuple-element.243, s32[]{:T(128)} %get-tuple-element.242, bf16[6,3,16,1344]{3,2,1,0:T(8,128)(2,1)S(1)} %get-tuple-element.260, f32[1344]{0:T(1024)S(1)} %dynamic-slice_reduce_fusion.4, f32[1344,1344]{1,0:T(8,128)} %not_convert_fusion.2, f32[3]{0:T(128)S(1)} %fusion.36, ...), kind=kOutput, calls=%fused_computation.10.clone.1 | convolution fusion | flops 205922304 | bytes 15563264 | tf_op jit(solution)/shard_map/while/body/eval_jaxpr/dot_general | solution.py:114
  269.9 9.3 %copy.89 = f32[1,18,16,1344]{1,2,0,3:T(8,128)} copy(f32[1,18,16,1344]{3,2,1,0:T(8,128)} %bitcast.159) | data formatting | bytes 3096576 | tf_op jit(solution)/shard_map/reshape;reshape | solution.py:137
  279.2 13.0 %reshape.326 = f32[32,1,12096]{2,1,0:T(1,128)} reshape(f32[1344,1,16,18]{3,2,1,0:T(8,128)} %bitcast.141) | data formatting | bytes 3096576
  292.2 6.4 %all-to-all-start.2 = ((f32[32,1,12096]{2,1,0:T(1,128)}), f32[32,1,12096]{2,1,0:T(1,128)S(1)}, u32[]{:S(2)}, u32[]{:S(2)}) async-start(f32[32,1,12096]{2,1,0:T(1,128)} %reshape.326), calls=%async_computation.2 | async-start | bytes 3112960 | tf_op jit(solution)/shard_map/all_to_all | solution.py:136
  298.6 9.3 %copy.92 = f32[1,18,16,1344]{1,2,0,3:T(8,128)} copy(f32[1,18,16,1344]{3,2,1,0:T(8,128)} %bitcast.160) | data formatting | bytes 3096576 | tf_op jit(solution)/shard_map/reshape | solution.py:134
  307.9 13.0 %reshape.328 = f32[32,1,12096]{2,1,0:T(1,128)} reshape(f32[1344,1,16,18]{3,2,1,0:T(8,128)} %bitcast.142) | data formatting | bytes 3096576
  320.9 12.6 %all-to-all-done.2 = f32[32,1,12096]{2,1,0:T(1,128)S(1)} async-done(((f32[32,1,12096]{2,1,0:T(1,128)}), f32[32,1,12096]{2,1,0:T(1,128)S(1)}, u32[]{:S(2)}, u32[]{:S(2)}) %all-to-all-start.2) | async-done | bytes 1548320 | tf_op jit(solution)/shard_map/all_to_all | solution.py:136
  333.5 6.5 %all-to-all-start.3 = ((f32[32,1,12096]{2,1,0:T(1,128)}), f32[32,1,12096]{2,1,0:T(1,128)}, u32[]{:S(2)}, u32[]{:S(2)}) async-start(f32[32,1,12096]{2,1,0:T(1,128)} %reshape.328), calls=%async_computation.3 | async-start | bytes 3112960 | tf_op jit(solution)/shard_map/all_to_all | solution.py:143
  340.5 4.5 reduce.17
  345.1 14.1 %reshape.327 = f32[1344,1,16,18]{3,2,1,0:T(8,128)} reshape(f32[32,12096]{1,0:T(8,128)S(1)} %reduce.17) | data formatting | bytes 3096576
  359.2 11.2 %copy.97 = f32[1,18,16,32,42]{4,3,2,1,0:T(8,128)} copy(f32[1,18,16,32,42]{1,2,4,3,0:T(8,128)} %bitcast.143) | data formatting | bytes 3096576 | tf_op jit(solution)/shard_map/all_to_all | solution.py:136
  370.4 7.2 %copy.91 = f32[1,32,18,16,42]{4,3,2,1,0:T(8,128)} copy(f32[1,32,18,16,42]{4,1,3,2,0:T(8,128)} %bitcast.154) | data formatting | bytes 3096576 | tf_op jit(solution)/shard_map/all_to_all | solution.py:136
  377.6 3.3 reduce_sum.86
  382.2 6.9 %reduce.18 = f32[32,12096]{1,0:T(8,128)} reduce(f32[32,1,12096]{2,1,0:T(1,128)} %all-to-all-done.3, f32[]{:T(128)} %broadcast.214), dimensions={1}, to_apply=%all_to_all.53.reduce_sub_computation | reduce | bytes 3096580 | tf_op jit(solution)/shard_map/all_to_all | solution.py:143
  389.2 15.0 %reshape.329 = f32[1344,1,16,18]{3,2,1,0:T(8,128)} reshape(f32[32,12096]{1,0:T(8,128)} %reduce.18) | data formatting | bytes 3096576
  404.2 11.3 %copy.98 = f32[1,18,16,32,42]{4,3,2,1,0:T(8,128)} copy(f32[1,18,16,32,42]{1,2,4,3,0:T(8,128)} %bitcast.144) | data formatting | bytes 3096576 | tf_op jit(solution)/shard_map/all_to_all | solution.py:143
  415.5 5.2 %copy.94 = f32[1,32,18,16,42]{4,3,2,1,0:T(8,128)S(1)} copy(f32[1,32,18,16,42]{4,1,3,2,0:T(8,128)} %bitcast.155) | data formatting | bytes 3096576 | tf_op jit(solution)/shard_map/all_to_all | solution.py:143
  420.7 7.0 %fusion.25 = (f32[42,16]{0,1:T(8,128)S(1)}, f32[42,48,4,16]{0,3,2,1:T(8,128)}) fusion(f32[1,42,48,4,3,16]{1,5,4,3,2,0:T(8,128)S(1)} %bitcast.145, f32[1,42,48,4,3,16]{1,5,4,3,2,0:T(8,128)} %bitcast.138, f32[42,48,4,16]{0,3,2,1:T(8,128)S(1)} %copy-done.9), kind=kLoop, calls=%fused_computation.59 | loop fusion | flops 1418592 | bytes 4131456 | tf_op jit(solution)/shard_map/reduce_sum | solution.py:158
  427.7 25.8 %all-reduce = (f32[1,16,42]{2,1,0:T(8,128)S(1)}, f32[1,16,42]{2,1,0:T(8,128)S(1)}) all-reduce(f32[1,16,42]{2,1,0:T(8,128)S(1)} %bitcast_multiply_fusion.1, f32[1,16,42]{2,1,0:T(8,128)S(1)} %multiply_bitcast_fusion), channel_id=1, replica_groups=mesh['river'=8,'leaf'=32] {'river'}, use_global_device_ids=true, to_apply=%region_9.10 | all-reduce | flops 1344 | bytes 10752 | tf_op jit(solution)/shard_map/psum | solution.py:159
  454.8 8.0 %subtract_maximum_fusion = f32[1,42,48,4,3,16]{1,5,4,3,2,0:T(8,128)} fusion(f32[1,42,48,4,3,16]{1,5,4,3,2,0:T(8,128)} %bitcast.139, f32[1,42,48,4,3,16]{1,5,4,3,2,0:T(8,128)} %bitcast.146, f32[42,48,4,16]{0,3,2,1:T(8,128)} %get-tuple-element.117), kind=kLoop, calls=%fused_computation.26 | loop fusion | flops 1161216 | bytes 5160960 | tf_op jit(solution)/shard_map/max | solution.py:156
  462.8 5.9 %copy.96 = f32[1,42,9216]{2,0,1:T(1,128)} copy(f32[1,42,9216]{1,2,0:T(8,128)} %bitcast.153) | data formatting | bytes 3096576
  468.7 1.6 fusion.16
  470.3 2.4 copy.95
  (108 shorter events, 15.8 us)
Async XLA Ops:
  0.6 61.9 %copy-start = (s32[1,12]{1,0:T(1,128)S(1)}, s32[1,12]{1,0:T(1,128)}, u32[]{:S(2)}) copy-start(s32[1,12]{1,0:T(1,128)} %param.20) | copy-start | bytes 148
  2.2 36.0 %copy-start.6 = (f32[1,42,3072]{1,2,0:T(8,128)}, f32[1,42,3072]{1,2,0:T(8,128)S(1)}, u32[]{:S(2)}) copy-start(f32[1,42,3072]{1,2,0:T(8,128)S(1)} %copy.81) | copy-start | bytes 1548292
  17.6 20.6 %copy-start.10 = (f32[42,48,16]{0,2,1:T(8,128)}, f32[42,48,16]{0,2,1:T(8,128)S(1)}, u32[]{:S(2)}) copy-start(f32[42,48,16]{0,2,1:T(8,128)S(1)} %reduce_sum.83) | copy-start | bytes 387076
  21.3 30.7 %all-to-all-start.1 = ((bf16[32,2,2016]{2,1,0:T(2,128)(2,1)}), bf16[32,2,2016]{2,1,0:T(2,128)(2,1)S(1)}, u32[]{:S(2)}, u32[]{:S(2)}) async-start(bf16[32,2,2016]{2,1,0:T(2,128)(2,1)} %reshape.324), calls=%async_computation.1 | async-start | bytes 524288 | tf_op jit(solution)/shard_map/all_to_all | solution.py:87
  41.4 1.2 copy-start.8
  41.5 2.9 copy-start.4
  41.5 2.9 copy-start.16
  46.5 15.8 %copy-start.17 = (s32[52]{0:T(128)S(1)}, s32[52]{0:T(128)}, u32[]{:S(2)}) copy-start(s32[52]{0:T(128)} %param.18) | copy-start | bytes 628
  46.5 16.8 %copy-start.2 = (s32[1,12]{1,0:T(1,128)S(1)}, s32[1,12]{1,0:T(1,128)}, u32[]{:S(2)}) copy-start(s32[1,12]{1,0:T(1,128)} %param.21) | copy-start | bytes 148
  52.0 12.1 %copy-start.15 = (s32[1344,2]{0,1:T(2,128)S(1)}, s32[1344,2]{0,1:T(2,128)}, u32[]{:S(2)}) copy-start(s32[1344,2]{0,1:T(2,128)} %param.17) | copy-start | bytes 32260
  52.0 28.9 %all-to-all-start = ((bf16[32,2,6048]{2,1,0:T(2,128)(2,1)}), bf16[32,2,6048]{2,1,0:T(2,128)(2,1)S(1)}, u32[]{:S(2)}, u32[]{:S(2)}) async-start(bf16[32,2,6048]{2,1,0:T(2,128)(2,1)} %reshape.322), calls=%async_computation | async-start | bytes 1572864 | tf_op jit(solution)/shard_map/all_to_all | solution.py:97
  97.6 14.3 %copy-start.3 = (f32[1344,1344]{1,0:T(8,128)}, f32[1344,1344]{1,0:T(8,128)S(1)}, u32[]{:S(2)}) copy-start(f32[1344,1344]{1,0:T(8,128)S(1)} %sign_convert_fusion.2) | copy-start | bytes 21676036 | tf_op jit(solution)/shard_map/while
  127.1 14.3 %copy-start.3 = (f32[1344,1344]{1,0:T(8,128)}, f32[1344,1344]{1,0:T(8,128)S(1)}, u32[]{:S(2)}) copy-start(f32[1344,1344]{1,0:T(8,128)S(1)} %sign_convert_fusion.2) | copy-start | bytes 21676036 | tf_op jit(solution)/shard_map/while
  156.6 14.3 %copy-start.3 = (f32[1344,1344]{1,0:T(8,128)}, f32[1344,1344]{1,0:T(8,128)S(1)}, u32[]{:S(2)}) copy-start(f32[1344,1344]{1,0:T(8,128)S(1)} %sign_convert_fusion.2) | copy-start | bytes 21676036 | tf_op jit(solution)/shard_map/while
  186.1 14.3 %copy-start.3 = (f32[1344,1344]{1,0:T(8,128)}, f32[1344,1344]{1,0:T(8,128)S(1)}, u32[]{:S(2)}) copy-start(f32[1344,1344]{1,0:T(8,128)S(1)} %sign_convert_fusion.2) | copy-start | bytes 21676036 | tf_op jit(solution)/shard_map/while
  215.6 14.3 %copy-start.3 = (f32[1344,1344]{1,0:T(8,128)}, f32[1344,1344]{1,0:T(8,128)S(1)}, u32[]{:S(2)}) copy-start(f32[1344,1344]{1,0:T(8,128)S(1)} %sign_convert_fusion.2) | copy-start | bytes 21676036 | tf_op jit(solution)/shard_map/while
  245.1 14.3 %copy-start.3 = (f32[1344,1344]{1,0:T(8,128)}, f32[1344,1344]{1,0:T(8,128)S(1)}, u32[]{:S(2)}) copy-start(f32[1344,1344]{1,0:T(8,128)S(1)} %sign_convert_fusion.2) | copy-start | bytes 21676036 | tf_op jit(solution)/shard_map/while
  292.2 41.3 %all-to-all-start.2 = ((f32[32,1,12096]{2,1,0:T(1,128)}), f32[32,1,12096]{2,1,0:T(1,128)S(1)}, u32[]{:S(2)}, u32[]{:S(2)}) async-start(f32[32,1,12096]{2,1,0:T(1,128)} %reshape.326), calls=%async_computation.2 | async-start | bytes 3112960 | tf_op jit(solution)/shard_map/all_to_all | solution.py:136
  333.5 48.7 %all-to-all-start.3 = ((f32[32,1,12096]{2,1,0:T(1,128)}), f32[32,1,12096]{2,1,0:T(1,128)}, u32[]{:S(2)}, u32[]{:S(2)}) async-start(f32[32,1,12096]{2,1,0:T(1,128)} %reshape.328), calls=%async_computation.3 | async-start | bytes 3112960 | tf_op jit(solution)/shard_map/all_to_all | solution.py:143
  377.6 3.4 copy-start.7
  377.6 3.4 copy-start.11
  415.5 5.2 %copy-start.9 = (f32[42,48,4,16]{0,3,2,1:T(8,128)S(1)}, f32[42,48,4,16]{0,3,2,1:T(8,128)}, u32[]{:S(2)}) copy-start(f32[42,48,4,16]{0,3,2,1:T(8,128)} %copy-done.8) | copy-start | bytes 1548292
  420.7 7.0 %copy-start.5 = (f32[1,32,18,16,42]{4,3,2,1,0:T(8,128)}, f32[1,32,18,16,42]{4,3,2,1,0:T(8,128)S(1)}, u32[]{:S(2)}) copy-start(f32[1,32,18,16,42]{4,3,2,1,0:T(8,128)S(1)} %copy.94) | copy-start | bytes 4644868
  420.7 7.0 %copy-start.14 = (f32[1,16,42]{2,1,0:T(8,128)S(1)}, f32[1,16,42]{2,1,0:T(8,128)}, u32[]{:S(2)}) copy-start(f32[1,16,42]{2,1,0:T(8,128)} %get-tuple-element.151) | copy-start | bytes 8068
  420.7 32.8 %copy-start.13 = (f32[1,16,42]{2,1,0:T(8,128)S(1)}, f32[1,16,42]{2,1,0:T(8,128)}, u32[]{:S(2)}) copy-start(f32[1,16,42]{2,1,0:T(8,128)} %param.14) | copy-start | bytes 8068
  462.8 5.9 %copy-start.12 = (f32[42,48,16]{0,2,1:T(8,128)S(1)}, f32[42,48,16]{0,2,1:T(8,128)}, u32[]{:S(2)}) copy-start(f32[42,48,16]{0,2,1:T(8,128)} %get-tuple-element.118) | copy-start | bytes 387076
  462.8 9.8 %copy-start.1 = (s32[1,12]{1,0:T(1,128)S(1)}, s32[1,12]{1,0:T(1,128)}, u32[]{:S(2)}) copy-start(s32[1,12]{1,0:T(1,128)} %param.20) | copy-start | bytes 148
where the time goes:
time: 481 us; the launch traced here: 473 us
  local copies, waits for them, and re-layouts  161 us (33%)
  matrix products  115 us (24%)
  other arithmetic  82.8 us (17%)
  blocking collectives  41.1 us (9%)
  starting transfers between devices  34.3 us (7%)
  waiting for transfers between devices  25.2 us (5%)
  loops' own time  12.5 us (3%)
    unnamed x46, local copies, waits for them, and re-layouts  86.4 us
    dot_general x6, matrix products, group_values(): lax.dot_general(one_group, payoffs, (((2,), (2,)), ((0,), (0,))), preferr...  62 us
    dot_general x6, matrix products, group_values(): lax.dot_general(zero_group, payoffs, (((1,), (1,)), ((), ())), preferred_...  53.1 us
    convert_element_type x6, other arithmetic, card_intersection(): return jnp.logical_not(shared).astype(jnp.float32)  32.1 us
    psum x1, blocking collectives, local(): lax.psum((jnp.sum(turn_share * line_zero, axis=0), jnp.sum(line_one, axis...  25.8 us
    all_to_all x3, local copies, waits for them, and re-layouts, local(): lax.all_to_all(zero_values.reshape(line_count, per_device, subgames, all_...  18.9 us
    all_to_all x2, local copies, waits for them, and re-layouts, local(): lax.all_to_all(one_values, 'leaf', split_axis=3, concat_axis=1, tiled=True)  16.5 us
    psum x1, blocking collectives, local(): turn_total = lax.psum(jnp.sum(turn_regret, axis=0), 'river')  15.2 us
  transfers between devices with their start and end apart: 4, of which 2 were waited for; matrix products, arithmetic and copies ran while one was open for 18% of the time, Pallas kernels for 0%

commit v1 on v0

v1 whole, which is shorter than its diff:
```python
import jax
import jax.numpy as jnp
from jax import lax
from jax.experimental import pallas as pl
from jax.experimental.pallas import tpu as pltpu
from jax.sharding import PartitionSpec as P

MESH = pl.DeviceIdType.MESH
F32 = jnp.float32
BF16 = jnp.bfloat16
RIVERS = 48
MOVES_ZERO = 4
MOVES_ONE = 3
SUBGAMES = 16
WORKERS = 24
PEERS = 32
HP = 48
KP = PEERS * HP
MB = 384
CHANCE = 1.0 / 44.0


def worker_leaf(w):
    z = w // 3
    x = lax.rem(w - 3 * z + 1 + z, 4)
    return 4 * z + x


def leaf_worker(leaf):
    z = leaf // 4
    x = leaf - 4 * z
    k = lax.rem(x - 1 - z + 12, 4)
    return k, 3 * z + k


def lanes(rows):
    return lax.broadcasted_iota(jnp.int32, (rows, 128), 1)


def gather_lanes(x, index):
    return jnp.take_along_axis(x, index, axis=1, mode="promise_in_bounds")


def roll_half(x):
    return pltpu.roll(x, 64, 1)


def action_sum(x, lane):
    x = x + gather_lanes(x, (lane & 64) | ((lane + 16) & 63))
    return x + gather_lanes(x, (lane & 64) | ((lane + 32) & 63))


def split_moves(tiles, lane):
    slot, sub = lane // 16, lane % 16
    out = []
    for b in range(MOVES_ONE):
        group = (3 * (slot - b + 8)) % 8
        tile = (3 * group + b) // 8
        picked = jnp.where(tile == 0, tiles[0], jnp.where(tile == 1, tiles[1], tiles[2]))
        out.append(gather_lanes(picked, ((3 * slot + b) % 8) * 16 + sub))
    return out


def join_moves(parts, lane):
    slot, sub = lane // 16, lane % 16
    moved = []
    for b in range(MOVES_ONE):
        group = (3 * (slot - b + 8)) % 8
        moved.append(gather_lanes(parts[b], group * 16 + sub))
    out = []
    for v in range(3):
        b = (8 * v + slot) % 3
        out.append(jnp.where(b == 0, moved[0], jnp.where(b == 1, moved[1], moved[2])))
    return out


def tile_selector():
    sub = lax.broadcasted_iota(jnp.int32, (SUBGAMES, 128), 0)
    lane = lanes(SUBGAMES)
    return (lane % SUBGAMES == sub).astype(F32)


def to_lanes(x):
    return lax.dot_general(
        x,
        tile_selector(),
        (((0,), (0,)), ((), ())),
        precision=lax.Precision.HIGHEST,
        preferred_element_type=F32,
    )


def zero_shares(rz, w, lane):
    x = rz[:, pl.ds(128 * w, 128)]
    return x, x / action_sum(x, lane)


def one_shares(ro, w, lane):
    tiles = [ro[:, pl.ds(384 * w + 128 * v, 128)] for v in range(3)]
    regrets = split_moves(tiles, lane)
    scale = 1.0 / (regrets[0] + regrets[1] + regrets[2])
    return regrets, [r * scale for r in regrets]


def prep_kernel(rz, ro, range_zero, range_one, turn_regret, turn_total, y):
    hands = rz.shape[0]
    lane = lanes(hands)
    low = lane < 64
    weight_zero = to_lanes(range_zero[...] * (turn_regret[...] / turn_total[...]))
    weight_one = to_lanes(range_one[...])

    def step(w, carry):
        _, zs = zero_shares(rz, w, lane)
        _, os = one_shares(ro, w, lane)
        z = weight_zero * zs
        o = [weight_one * s for s in os]
        packed = (
            jnp.where(low, z, roll_half(o[0])),
            jnp.where(low, o[1], roll_half(o[2])),
            jnp.where(low, roll_half(z), o[0]),
            jnp.where(low, roll_half(o[1]), o[2]),
        )
        for k in range(4):
            y[w, k, 32:48] = jnp.zeros((16, 128), BF16)
            y[w, k, 0:hands] = packed[k].astype(BF16)
        return carry

    lax.fori_loop(0, WORKERS, step, 0)


def entry_barrier(line, leaf):
    barrier = pltpu.get_barrier_semaphore()

    def greet(k, carry):
        peer = lax.rem(leaf + k, PEERS)
        pl.semaphore_signal(barrier, inc=1, device_id=(line, peer), device_id_type=MESH)
        return carry

    lax.fori_loop(1, PEERS, greet, 0)
    pl.semaphore_wait(barrier, PEERS - 1)


def forward_kernel(y, recv, send_sem, recv_sem, local_sem):
    line, leaf = lax.axis_index("river"), lax.axis_index("leaf")
    k_self, w_self = leaf_worker(leaf)
    is_worker = k_self < 3
    entry_barrier(line, leaf)
    first = 3 * (leaf // 4)

    def copy(w, peer):
        return pltpu.make_async_remote_copy(
            src_ref=y.at[w],
            dst_ref=recv.at[leaf],
            send_sem=send_sem.at[w],
            recv_sem=recv_sem.at[leaf],
            device_id=(line, peer),
            device_id_type=MESH,
        )

    def start(k, carry):
        w = lax.rem(first + k, WORKERS)
        peer = worker_leaf(w)

        @pl.when(peer != leaf)
        def _():
            copy(w, peer).start()

        return carry

    lax.fori_loop(0, WORKERS, start, 0)

    @pl.when(is_worker)
    def _():
        own = pltpu.make_async_copy(y.at[w_self], recv.at[leaf], local_sem)
        own.start()
        own.wait()

        def arrive(k, carry):
            source = lax.rem(leaf + k, PEERS)
            pltpu.make_async_remote_copy(
                src_ref=y.at[0],
                dst_ref=recv.at[source],
                send_sem=send_sem.at[0],
                recv_sem=recv_sem.at[source],
                device_id=(line, source),
                device_id_type=MESH,
            ).wait_recv()
            return carry

        lax.fori_loop(1, PEERS, arrive, 0)

    def sent(k, carry):
        w = lax.rem(first + k, WORKERS)
        peer = worker_leaf(w)

        @pl.when(peer != leaf)
        def _():
            copy(w, peer).wait_send()

        return carry

    lax.fori_loop(0, WORKERS, sent, 0)


def backward_kernel(out, back, send_sem, recv_sem, local_sem):
    line, leaf = lax.axis_index("river"), lax.axis_index("leaf")
    k_self, w_self = leaf_worker(leaf)
    is_worker = k_self < 3
    entry_barrier(line, leaf)
    first = 3 * (leaf // 4)

    def copy(peer):
        return pltpu.make_async_remote_copy(
            src_ref=out.at[peer],
            dst_ref=back.at[w_self],
            send_sem=send_sem.at[peer],
            recv_sem=recv_sem.at[w_self],
            device_id=(line, peer),
            device_id_type=MESH,
        )

    @pl.when(is_worker)
    def _():
        def start(k, carry):
            copy(lax.rem(leaf + k, PEERS)).start()
            return carry

        lax.fori_loop(1, PEERS, start, 0)
        own = pltpu.make_async_copy(out.at[leaf], back.at[w_self], local_sem)
        own.start()
        own.wait()

    def arrive(k, carry):
        w = lax.rem(first + k, WORKERS)
        peer = worker_leaf(w)

        @pl.when(peer != leaf)
        def _():
            pltpu.make_async_remote_copy(
                src_ref=out.at[0],
                dst_ref=back.at[w],
                send_sem=send_sem.at[0],
                recv_sem=recv_sem.at[w],
                device_id=(line, peer),
                device_id_type=MESH,
            ).wait_recv()

        return carry

    lax.fori_loop(0, WORKERS, arrive, 0)

    @pl.when(is_worker)
    def _():
        def sent(k, carry):
            copy(lax.rem(leaf + k, PEERS)).wait_send()
            return carry

        lax.fori_loop(1, PEERS, sent, 0)


def leaf_scales(pots, kinds, rows):
    action = (lanes(rows) // SUBGAMES) % MOVES_ZERO
    show, fold = [], []
    for b in range(MOVES_ONE):
        s = jnp.zeros((rows, 128), F32)
        f = jnp.zeros((rows, 128), F32)
        for a in range(MOVES_ZERO):
            pot = pots[0, a * MOVES_ONE + b].astype(F32)
            kind = kinds[0, a * MOVES_ONE + b]
            here = action == a
            s = jnp.where(here, jnp.where(kind == 0, pot, 0.0), s)
            f = jnp.where(here, jnp.where(kind == 0, 0.0, jnp.where(kind == 1, pot, -pot)), f)
        show.append(s)
        fold.append(f)
    return show, fold


def column(rows, select):
    return lax.dot_general(
        rows, select, (((0,), (0,)), ((), ())), preferred_element_type=F32
    )


def blocks_kernel(recv, cards, ranks, dealt, pots, kinds, out, x, mat, dis, col, inc):
    leaf = lax.axis_index("leaf")
    k_self, w_self = leaf_worker(leaf)

    @pl.when(k_self < 3)
    def _():
        low = lanes(8) < 64
        one_row = (lax.broadcasted_iota(jnp.int32, (8, 128), 0))
        pick = lambda r, scale: jnp.where(one_row == r, scale, 0.0).astype(BF16)
        card_rows = cards[...].astype(BF16)
        first = column(card_rows, pick(0, 1.0))
        second = column(card_rows, pick(1, 1.0))
        board = [dealt[k].astype(F32) for k in range(4)]
        usable = (first < 52.0) & (second < 52.0)
        for k in range(4):
            usable = usable & (first != board[k]) & (second != board[k])
        valid = []
        for c in range(2):
            river = dealt[4 + 2 * w_self + c].astype(F32)
            ok = usable & (first != river) & (second != river)
            valid.append(ok.astype(F32))
        card = lanes(KP).astype(F32)
        inc[...] = ((first == card) | (second == card)).astype(BF16)
        rank_rows = ranks[...]
        high_rows = jnp.floor(rank_rows * (1.0 / 64.0))
        low_rows = rank_rows - 64.0 * high_rows
        for c in range(2):
            col[c] = column(high_rows.astype(BF16), pick(c, 64.0)) + column(
                low_rows.astype(BF16), pick(c, 1.0)
            )
            col[2 + c] = valid[c]
            vb = valid[c].astype(BF16)
            for k in range(2):
                x[:, pl.ds(256 * c + 128 * k, 128)] = (
                    recv[:, 2 * c + k].reshape(KP, 128) * vb
                )
        show, fold = leaf_scales(pots, kinds, 8)
        show = [s[0:1] for s in show]
        fold = [f[0:1] for f in fold]
        low_row = low[0:1]
        show_mix = jnp.where(low_row, show[1], show[2])
        fold_mix = jnp.where(low_row, fold[1], fold[2])

        def block(i, carry):
            rows = pl.ds(pl.multiple_of(i * MB, MB), MB)
            for j in range(KP // 128):
                js = pl.ds(128 * j, 128)
                shared = lax.dot_general(
                    inc[rows], inc[js], (((1,), (1,)), ((), ())), preferred_element_type=F32
                )
                apart = jnp.maximum(1.0 - shared, 0.0)
                dis[:, js] = apart.astype(BF16)
                for c in range(2):
                    gap = col[c, rows] - rank_rows[c : c + 1, 128 * j : 128 * j + 128]
                    sign = jnp.minimum(jnp.maximum(gap, -1.0), 1.0)
                    mat[c, :, js] = (sign * apart).astype(BF16)
            acts, shows, folds = [], [], []
            for c in range(2):
                xc = x[:, pl.ds(256 * c, 256)]
                s = jnp.dot(mat[c], xc, preferred_element_type=F32)
                d = jnp.dot(dis[...], xc, preferred_element_type=F32)
                v = col[2 + c, rows]
                s0, s1 = s[:, :128] * v, s[:, 128:] * v
                d0, d1 = d[:, :128] * v, d[:, 128:] * v
                mixed = s1 * show_mix + d1 * fold_mix
                act = s0 * show[0] + d0 * fold[0] + mixed + roll_half(mixed)
                acts.append(jnp.where(low_row, s0, act))
                folds.append(d0)
            tiles = (acts[0], acts[1], jnp.where(low_row, folds[0], roll_half(folds[1])))
            for k in range(3):
                out[pl.ds(i * (MB // HP), MB // HP), k] = tiles[k].reshape(MB // HP, HP, 128)
            return carry

        lax.fori_loop(0, KP // MB, block, 0)


def update_kernel(rz, ro, back, pots, kinds, new_rz, new_ro, lines):
    hands = rz.shape[0]
    lane = lanes(hands)
    low = lane < 64
    show, fold = leaf_scales(pots, kinds, hands)

    def step(w, carry):
        sum_zero, sum_one = carry
        r, zs = zero_shares(rz, w, lane)
        regrets, os = one_shares(ro, w, lane)
        t0, t1, dz = back[w, 0, 0:hands], back[w, 1, 0:hands], back[w, 2, 0:hands]
        act = jnp.where(low, roll_half(t0), t1)
        sz = jnp.where(low, t0, roll_half(t1))
        node = action_sum(zs * act, lane)
        new_rz[:, pl.ds(128 * w, 128)] = jnp.maximum(r + act - node, 0.0)
        leaf_one = [show[b] * sz - fold[b] * dz for b in range(MOVES_ONE)]
        node_one = os[0] * leaf_one[0] + os[1] * leaf_one[1] + os[2] * leaf_one[2]
        new = [jnp.maximum(regrets[b] + leaf_one[b] - node_one, 0.0) for b in range(MOVES_ONE)]
        native = join_moves(new, lane)
        for v in range(3):
            new_ro[:, pl.ds(384 * w + 128 * v, 128)] = native[v]
        return (sum_zero + node, sum_one + node_one)

    zero = jnp.zeros((hands, 128), F32)
    sum_zero, sum_one = lax.fori_loop(0, WORKERS, step, (zero, zero))
    sum_zero = jnp.where(lane % 64 < SUBGAMES, sum_zero, 0.0)
    for k, total in enumerate((sum_zero, sum_one)):
        lines[k] = CHANCE * lax.dot_general(
            tile_selector(),
            total,
            (((1,), (1,)), ((), ())),
            precision=lax.Precision.HIGHEST,
            preferred_element_type=F32,
        )


VM = pl.BlockSpec(memory_space=pltpu.VMEM)
SM = pl.BlockSpec(memory_space=pltpu.SMEM)
LIMIT = 48 << 20


def exchange(kernel, identity, operand, shape, dtype, sends, recvs):
    return pl.pallas_call(
        kernel,
        out_shape=jax.ShapeDtypeStruct(shape, dtype),
        in_specs=[VM],
        out_specs=VM,
        scratch_shapes=[
            pltpu.SemaphoreType.DMA((sends,)),
            pltpu.SemaphoreType.DMA((recvs,)),
            pltpu.SemaphoreType.DMA,
        ],
        compiler_params=pltpu.CompilerParams(
            collective_id=identity, has_side_effects=True, vmem_limit_bytes=LIMIT
        ),
    )(operand)


def local(
    range_zero,
    range_one,
    turn_regret,
    river_regret_zero,
    river_regret_one,
    hand_cards,
    dealt_cards,
    hand_ranks,
    leaf_pots,
    leaf_kinds,
):
    hands = range_zero.shape[1]
    rz = river_regret_zero[0]
    ro = river_regret_one[0]
    tr = turn_regret[0]
    params = pltpu.CompilerParams(vmem_limit_bytes=LIMIT)
    turn_total = lax.psum(tr, "river")
    y = pl.pallas_call(
        prep_kernel,
        out_shape=jax.ShapeDtypeStruct((WORKERS, 4, HP, 128), BF16),
        in_specs=[VM] * 6,
        out_specs=VM,
        compiler_params=params,
    )(rz, ro, range_zero, range_one, tr, turn_total)
    recv = exchange(
        forward_kernel, 1, y, (PEERS, 4, HP, 128), BF16, WORKERS, PEERS
    )
    cards = jnp.pad(
        hand_cards.T.reshape(2, PEERS, hands), ((0, 0), (0, 0), (0, HP - hands)), constant_values=52
    ).reshape(2, KP)
    cards = jnp.pad(cards.astype(F32), ((0, 6), (0, 0)))
    _, w_self = leaf_worker(lax.axis_index("leaf"))
    w_self = jnp.minimum(w_self, WORKERS - 1)
    ranks = lax.dynamic_slice_in_dim(hand_ranks, 2 * w_self, 2, 0)
    ranks = jnp.pad(ranks.reshape(2, PEERS, hands), ((0, 0), (0, 0), (0, HP - hands))).reshape(2, KP)
    ranks = jnp.pad(ranks.astype(F32), ((0, 6), (0, 0)))
    out = pl.pallas_call(
        blocks_kernel,
        out_shape=jax.ShapeDtypeStruct((PEERS, 3, HP, 128), F32),
        in_specs=[VM, VM, VM, SM, SM, SM],
        out_specs=VM,
        scratch_shapes=[
            pltpu.VMEM((KP, 512), BF16),
            pltpu.VMEM((2, MB, KP), BF16),
            pltpu.VMEM((MB, KP), BF16),
            pltpu.VMEM((4, KP, 128), F32),
            pltpu.VMEM((KP, 128), BF16),
        ],
        compiler_params=params,
    )(recv, cards, ranks, dealt_cards, leaf_pots, leaf_kinds)
    back = exchange(
        backward_kernel, 2, out, (WORKERS, 3, HP, 128), F32, PEERS, WORKERS
    )
    new_rz, new_ro, lines = pl.pallas_call(
        update_kernel,
        out_shape=(
            jax.ShapeDtypeStruct(rz.shape, F32),
            jax.ShapeDtypeStruct(ro.shape, F32),
            jax.ShapeDtypeStruct((2, SUBGAMES, hands), F32),
        ),
        in_specs=[VM, VM, VM, SM, SM],
        out_specs=(VM, VM, VM),
        compiler_params=params,
    )(rz, ro, back, leaf_pots, leaf_kinds)
    line_zero = lines[0]
    share = tr / turn_total
    roots = lax.psum(jnp.stack([share * line_zero, lines[1]]), "river")
    new_turn = jnp.maximum(tr + line_zero - roots[0], 0.0)
    return (new_turn[None], new_rz[None], new_ro[None], roots)


def solution(mesh):
    placed = (
        P(None, "leaf"),
        P(None, "leaf"),
        P("river", None, "leaf"),
        P("river", "leaf", None),
        P("river", "leaf", None),
        P(),
        P(),
        P(),
        P("river", None),
        P("river", None),
    )
    return jax.shard_map(
        local,
        mesh=mesh,
        in_specs=placed,
        out_specs=(
            P("river", None, "leaf"),
            P("river", "leaf", None),
            P("river", "leaf", None),
            P(None, None, "leaf"),
        ),
        check_vma=False,
    )
```

time: 481 us -> 175 us (0.36)
  the two profiles are of different devices: /device:TPU:38 before, /device:TPU:6 now
where the time goes in v1:
time: 175 us; the launch traced here: 174 us
  Pallas kernels  123 us (70%)
  blocking collectives  41.5 us (24%)
  local copies, waits for them, and re-layouts  8.27 us (5%)
    pallas_call x2, Pallas kernels, exchange(): pl.pallas_call(kernel, out_shape=jax.ShapeDtypeStruct(shape, dtype), in_s...  96.5 us
    psum x1, blocking collectives, local(): roots = lax.psum(jnp.stack([share * line_zero, lines[1]]), 'river')  26.3 us
    psum x1, blocking collectives, local(): turn_total = lax.psum(tr, 'river')  15.2 us
    pallas_call x1, Pallas kernels, local(): pl.pallas_call(blocks_kernel, out_shape=jax.ShapeDtypeStruct((PEERS, 3, H...  11.3 us
    pallas_call x1, Pallas kernels, local(): pl.pallas_call(update_kernel, out_shape=(jax.ShapeDtypeStruct(rz.shape, F...  9.14 us
    unnamed x24, local copies, waits for them, and re-layouts  7.15 us
    pallas_call x1, Pallas kernels, local(): pl.pallas_call(prep_kernel, out_shape=jax.ShapeDtypeStruct((WORKERS, 4, H...  6.02 us

profile of v1, /device:TPU:6, one launch (start us, length us, event | category | flops | bytes accessed | tf_op | source)
XLA Modules:
  0.0 174.3 jit_solution(7156761430472762313)
XLA Ops:
  0.6 0.0 copy-start
  0.6 0.0 copy-start.8
  0.7 15.2 %psum.14.turn_total = f32[16,42]{1,0:T(8,128)S(1)} all-reduce(f32[16,42]{1,0:T(8,128)} %bitcast.23), channel_id=1, replica_groups=mesh['river'=8,'leaf'=32] {'river'}, use_global_device_ids=true, to_apply=%region_0.0 | all-reduce | flops 672 | bytes 5376 | tf_op jit(solution)/shard_map/psum | solution.py:435
  15.9 0.0 copy-done
  16.0 0.1 reshape.19
  16.1 0.1 convert_element_type.18
  16.2 0.8 reshape.18
  17.0 0.1 convert_element_type.16
  17.1 1.1 copy.21
  18.3 0.0 copy-start.2
  18.3 0.0 copy-start.3
  18.3 0.0 copy-start.4
  18.3 0.0 copy-done.8
  18.3 0.3 copy.20
  18.6 0.3 copy-done.2
  19.0 0.0 copy-done.3
  19.0 0.0 copy-done.4
  19.0 6.0 %shard_map.129.y = bf16[24,4,48,128]{3,2,1,0:T(8,128)(2,1)S(1)} custom-call(f32[42,3072]{1,0:T(8,128)S(1)} %bitcast.19, f32[42,9216]{1,0:T(8,128)S(1)} %bitcast.17, f32[16,42]{1,0:T(8,128)S(1)} %copy-done.3, f32[16,42]{1,0:T(8,128)S(1)} %copy-done.4, f32[16,42]{1,0:T(8,128)S(1)} %bitcast.24, f32[16,42]{1,0:T(8,128)S(1)} %psum.14.turn_total), custom_call_target="tpu_custom_call" | custom-call | tf_op jit(solution)/shard_map/pallas_call | solution.py:436
  25.1 0.0 copy-start.5
  25.1 0.0 copy-start.6
  25.1 0.0 copy-start.7
  25.1 37.1 %shard_map.130.recv = bf16[32,4,48,128]{3,2,1,0:T(8,128)(2,1)S(1)} custom-call(bf16[24,4,48,128]{3,2,1,0:T(8,128)(2,1)S(1)} %shard_map.129.y), custom_call_target="tpu_custom_call" | custom-call | tf_op jit(solution)/shard_map/pallas_call | solution.py:402
  62.2 0.0 copy-done.5
  62.2 0.0 copy-done.6
  62.2 0.0 copy-done.7
  62.2 11.3 %shard_map.131.out = f32[32,3,48,128]{3,2,1,0:T(8,128)S(1)} custom-call(bf16[32,4,48,128]{3,2,1,0:T(8,128)(2,1)S(1)} %shard_map.130.recv, f32[8,1536]{1,0:T(8,128)S(1)} %pad.15.cards, f32[8,1536]{1,0:T(8,128)S(1)} %pad.17.ranks, s32[52]{0:T(128)S(1)} %copy-done.7, s32[1,12]{1,0:T(1,128)S(1)} %copy-done.5, s32[1,12]{1,0:T(1,128)S(1)} %copy-done.6), custom_call_target="tpu_custom_call" | custom-call | tf_op jit(solution)/shard_map/pallas_call | solution.py:455
  73.5 59.4 %shard_map.132.back = f32[24,3,48,128]{3,2,1,0:T(8,128)S(1)} custom-call(f32[32,3,48,128]{3,2,1,0:T(8,128)S(1)} %shard_map.131.out), custom_call_target="tpu_custom_call" | custom-call | tf_op jit(solution)/shard_map/pallas_call | solution.py:402
  132.9 0.0 copy-start.1
  133.0 1.2 copy-done.1
  134.2 9.1 %shard_map.133 = (f32[42,3072]{1,0:T(8,128)S(1)}, f32[42,9216]{1,0:T(8,128)S(1)}, f32[2,16,42]{2,1,0:T(8,128)S(1)}) custom-call(f32[42,3072]{1,0:T(8,128)S(1)} %bitcast.20, f32[42,9216]{1,0:T(8,128)S(1)} %bitcast.18, f32[24,3,48,128]{3,2,1,0:T(8,128)} %copy-done.1, s32[1,12]{1,0:T(1,128)S(1)} %copy-done.5, s32[1,12]{1,0:T(1,128)S(1)} %copy-done.6), custom_call_target="tpu_custom_call" | custom-call | tf_op jit(solution)/shard_map/pallas_call | solution.py:472
  143.4 1.3 copy.14
  144.7 2.7 %copy.15 = f32[1,42,9216]{2,0,1:T(1,128)} copy(f32[1,42,9216]{2,1,0:T(8,128)S(1)} %bitcast.21) | data formatting | bytes 3096576
  147.4 26.3 %psum.15 = f32[2,16,42]{2,1,0:T(8,128)S(1)} all-reduce(f32[2,16,42]{2,1,0:T(8,128)S(1)} %pad_maximum_fusion), channel_id=1, replica_groups=mesh['river'=8,'leaf'=32] {'river'}, use_global_device_ids=true, to_apply=%region_1.2 | all-reduce | flops 1344 | bytes 10752 | tf_op jit(solution)/shard_map/psum | solution.py:485
  173.7 0.0 copy-start.9
  173.7 0.6 fusion
  174.3 0.0 copy-done.9
  (8 shorter events, 0.1 us)
Async XLA Ops:
  0.6 15.3 %copy-start = (s32[48,1344]{1,0:T(8,128)S(1)}, s32[48,1344]{1,0:T(8,128)}, u32[]{:S(2)}) copy-start(s32[48,1344]{1,0:T(8,128)} %param.17) | copy-start | bytes 774148
  0.6 17.7 %copy-start.8 = (f32[1,42,9216]{2,0,1:T(1,128)S(1)}, f32[1,42,9216]{2,0,1:T(1,128)}, u32[]{:S(2)}) copy-start(f32[1,42,9216]{2,0,1:T(1,128)} %param.14) | copy-start | bytes 4644868
  18.3 0.7 copy-start.2
  18.3 0.7 copy-start.3
  18.3 0.7 copy-start.4
  25.1 37.1 %copy-start.5 = (s32[1,12]{1,0:T(1,128)S(1)}, s32[1,12]{1,0:T(1,128)}, u32[]{:S(2)}) copy-start(s32[1,12]{1,0:T(1,128)} %pots.3) | copy-start | bytes 148
  25.1 37.1 %copy-start.6 = (s32[1,12]{1,0:T(1,128)S(1)}, s32[1,12]{1,0:T(1,128)}, u32[]{:S(2)}) copy-start(s32[1,12]{1,0:T(1,128)} %kinds.3) | copy-start | bytes 148
  25.1 37.1 %copy-start.7 = (s32[52]{0:T(128)S(1)}, s32[52]{0:T(128)}, u32[]{:S(2)}) copy-start(s32[52]{0:T(128)} %dealt.1) | copy-start | bytes 628
  132.9 1.2 copy-start.1
  173.7 0.6 copy-start.9

commit v2 on v1

v2 whole, which is shorter than its diff:
```python
import jax
import jax.numpy as jnp
from jax import lax
from jax.experimental import pallas as pl
from jax.experimental.pallas import tpu as pltpu
from jax.sharding import PartitionSpec as P

MESH = pl.DeviceIdType.MESH
F32 = jnp.float32
BF16 = jnp.bfloat16
RIVERS = 48
MOVES_ZERO = 4
MOVES_ONE = 3
SUBGAMES = 16
WORKERS = 24
PEERS = 32
HP = 48
KP = PEERS * HP
MB = 384
CHANCE = 1.0 / 44.0


def worker_leaf(w):
    z = w // 3
    x = lax.rem(w - 3 * z + 1 + z, 4)
    return 4 * z + x


def leaf_worker(leaf):
    z = leaf // 4
    x = leaf - 4 * z
    k = lax.rem(x - 1 - z + 12, 4)
    return k, 3 * z + k


def lanes(rows):
    return lax.broadcasted_iota(jnp.int32, (rows, 128), 1)


def gather_lanes(x, index):
    return jnp.take_along_axis(x, index, axis=1, mode="promise_in_bounds")


def roll_half(x):
    return pltpu.roll(x, 64, 1)


def action_sum(x, lane):
    x = x + gather_lanes(x, (lane & 64) | ((lane + 16) & 63))
    return x + gather_lanes(x, (lane & 64) | ((lane + 32) & 63))


def split_moves(tiles, lane):
    slot, sub = lane // 16, lane % 16
    out = []
    for b in range(MOVES_ONE):
        group = (3 * (slot - b + 8)) % 8
        tile = (3 * group + b) // 8
        picked = jnp.where(tile == 0, tiles[0], jnp.where(tile == 1, tiles[1], tiles[2]))
        out.append(gather_lanes(picked, ((3 * slot + b) % 8) * 16 + sub))
    return out


def join_moves(parts, lane):
    slot, sub = lane // 16, lane % 16
    moved = []
    for b in range(MOVES_ONE):
        group = (3 * (slot - b + 8)) % 8
        moved.append(gather_lanes(parts[b], group * 16 + sub))
    out = []
    for v in range(3):
        b = (8 * v + slot) % 3
        out.append(jnp.where(b == 0, moved[0], jnp.where(b == 1, moved[1], moved[2])))
    return out


def tile_selector():
    sub = lax.broadcasted_iota(jnp.int32, (SUBGAMES, 128), 0)
    lane = lanes(SUBGAMES)
    return (lane % SUBGAMES == sub).astype(F32)


def to_lanes(x):
    return lax.dot_general(
        x,
        tile_selector(),
        (((0,), (0,)), ((), ())),
        precision=lax.Precision.HIGHEST,
        preferred_element_type=F32,
    )


def zero_shares(rz, w, lane):
    x = rz[:, pl.ds(128 * w, 128)]
    return x, x / action_sum(x, lane)


def one_shares(ro, w, lane):
    tiles = [ro[:, pl.ds(384 * w + 128 * v, 128)] for v in range(3)]
    regrets = split_moves(tiles, lane)
    scale = 1.0 / (regrets[0] + regrets[1] + regrets[2])
    return regrets, [r * scale for r in regrets]


def leaf_scales(pots, kinds, rows):
    action = (lanes(rows) // SUBGAMES) % MOVES_ZERO
    show, fold = [], []
    for b in range(MOVES_ONE):
        s = jnp.zeros((rows, 128), F32)
        f = jnp.zeros((rows, 128), F32)
        for a in range(MOVES_ZERO):
            pot = pots[0, a * MOVES_ONE + b].astype(F32)
            kind = kinds[0, a * MOVES_ONE + b]
            here = action == a
            s = jnp.where(here, jnp.where(kind == 0, pot, 0.0), s)
            f = jnp.where(here, jnp.where(kind == 0, 0.0, jnp.where(kind == 1, pot, -pot)), f)
        show.append(s)
        fold.append(f)
    return show, fold


ONE_TOP = 64.0 * 0.001 * 1.005
CODE = 32760.0


def column(rows, select):
    return lax.dot_general(
        rows, select, (((0,), (0,)), ((), ())), preferred_element_type=F32
    )


def code(x):
    return x.astype(jnp.int32).astype(jnp.int16)


def nearest(x):
    return jnp.floor(x + 0.5)


def lead_kernel(
    rz_hbm,
    ro_hbm,
    range_zero,
    range_one,
    turn_regret,
    cards,
    ranks,
    dealt,
    pots,
    kinds,
    back,
    turn_total,
    rz,
    ro,
    turns,
    yz,
    yw,
    recv_z,
    recv_w,
    x,
    mat,
    col,
    inc,
    out,
    load_sem,
    turn_send,
    turn_recv,
    z_send,
    z_recv,
    w_send,
    w_recv,
    out_send,
    out_recv,
):
    line, leaf = lax.axis_index("river"), lax.axis_index("leaf")
    lines = turns.shape[0]
    k_self, w_self = leaf_worker(leaf)
    is_worker = k_self < 3
    hands = rz.shape[0]
    first_worker = 3 * (leaf // 4)

    loads = [
        pltpu.make_async_copy(rz_hbm, rz, load_sem.at[0]),
        pltpu.make_async_copy(ro_hbm, ro, load_sem.at[1]),
    ]
    for load in loads:
        load.start()

    barrier = pltpu.get_barrier_semaphore()

    def greet_leaf(k, carry):
        peer = lax.rem(leaf + k, PEERS)
        pl.semaphore_signal(barrier, inc=1, device_id=(line, peer), device_id_type=MESH)
        return carry

    def greet_line(k, carry):
        peer = lax.rem(line + k, lines)
        pl.semaphore_signal(barrier, inc=1, device_id=(peer, leaf), device_id_type=MESH)
        return carry

    lax.fori_loop(1, lines, greet_line, 0)
    lax.fori_loop(1, PEERS, greet_leaf, 0)
    pl.semaphore_wait(barrier, PEERS - 1 + lines - 1)

    def turn_copy(peer, slot):
        return pltpu.make_async_remote_copy(
            src_ref=turn_regret,
            dst_ref=turns.at[slot],
            send_sem=turn_send.at[peer],
            recv_sem=turn_recv.at[slot],
            device_id=(peer, leaf),
            device_id_type=MESH,
        )

    def turn_start(k, carry):
        turn_copy(lax.rem(line + k, lines), line).start()
        return carry

    lax.fori_loop(1, lines, turn_start, 0)
    turns[line] = turn_regret[...]

    def turn_wait(k, carry):
        peer = lax.rem(line + k, lines)
        turn_copy(peer, peer).wait_recv()
        return carry

    lax.fori_loop(1, lines, turn_wait, 0)
    total = turns[0]
    for t in range(1, lines):
        total = total + turns[t]
    turn_total[...] = total

    lane = lanes(hands)
    weight_zero = to_lanes(range_zero[...] * (turn_regret[...] / total))
    weight_one = to_lanes(range_one[...])
    show, fold = leaf_scales(pots, kinds, 8)
    show = [s[0:1] * (CODE / ONE_TOP) for s in show]
    fold = [f[0:1] * (CODE / ONE_TOP) for f in fold]
    for load in loads:
        load.wait()

    def z_copy(w, peer):
        return pltpu.make_async_remote_copy(
            src_ref=yz.at[w],
            dst_ref=recv_z.at[leaf],
            send_sem=z_send.at[w],
            recv_sem=z_recv.at[leaf],
            device_id=(line, peer),
            device_id_type=MESH,
        )

    def w_copy(w, peer):
        return pltpu.make_async_remote_copy(
            src_ref=yw.at[w],
            dst_ref=recv_w.at[leaf],
            send_sem=w_send.at[w],
            recv_sem=w_recv.at[leaf],
            device_id=(line, peer),
            device_id_type=MESH,
        )

    def prepare(k, carry):
        w = lax.rem(first_worker + k, WORKERS)
        _, zs = zero_shares(rz, w, lane)
        _, os = one_shares(ro, w, lane)
        yz[w, 32:48] = jnp.zeros((16, 128), BF16)
        yz[w, 0:hands] = (weight_zero * zs).astype(BF16)
        o = [(weight_one * s).astype(BF16).astype(F32) for s in os]
        for j, scale in enumerate((show, fold)):
            mixed = o[0] * scale[0] + o[1] * scale[1] + o[2] * scale[2]
            yw[w, j, 32:48] = jnp.zeros((16, 128), jnp.int16)
            yw[w, j, 0:hands] = code(nearest(mixed))
        peer = worker_leaf(w)

        @pl.when(peer != leaf)
        def _():
            z_copy(w, peer).start()
            w_copy(w, peer).start()

        @pl.when(peer == leaf)
        def _():
            recv_z[leaf] = yz[w]
            recv_w[leaf] = yw[w]

        return carry

    lax.fori_loop(0, WORKERS, prepare, 0)

    def out_copy(peer):
        return pltpu.make_async_remote_copy(
            src_ref=out.at[peer],
            dst_ref=back.at[w_self],
            send_sem=out_send.at[peer],
            recv_sem=out_recv.at[w_self],
            device_id=(line, peer),
            device_id_type=MESH,
        )

    @pl.when(is_worker)
    def _():
        low = lanes(8)[0:1] < 64
        one_row = lax.broadcasted_iota(jnp.int32, (8, 128), 0)
        pick = lambda r, scale: jnp.where(one_row == r, scale, 0.0).astype(BF16)
        card_rows = cards[...].astype(BF16)
        first = column(card_rows, pick(0, 1.0))
        second = column(card_rows, pick(1, 1.0))
        usable = (first < 52.0) & (second < 52.0)
        for k in range(4):
            board = dealt[k].astype(F32)
            usable = usable & (first != board) & (second != board)
        rivers = [dealt[4 + 2 * w_self + c].astype(F32) for c in range(2)]
        river = jnp.where(low, rivers[0], rivers[1])
        col[2] = (usable & (first != river) & (second != river)).astype(F32)
        inc[...] = ((first == lanes(KP).astype(F32)) | (second == lanes(KP).astype(F32))).astype(BF16)
        rank_rows = ranks[...]
        high_rows = jnp.floor(rank_rows * (1.0 / 64.0))
        low_rows = rank_rows - 64.0 * high_rows
        for c in range(2):
            col[c] = column(high_rows.astype(BF16), pick(c, 64.0)) + column(
                low_rows.astype(BF16), pick(c, 1.0)
            )

        def build(i, carry):
            rows = pl.ds(pl.multiple_of(i * MB, MB), MB)
            for j in range(KP // 128):
                js = pl.ds(128 * j, 128)
                shared = lax.dot_general(
                    inc[rows], inc[js], (((1,), (1,)), ((), ())), preferred_element_type=F32
                )
                apart = jnp.maximum(1.0 - shared, 0.0)
                mat[2, rows, js] = apart.astype(BF16)
                for c in range(2):
                    gap = col[c, rows] - ranks[c : c + 1, js]
                    sign = jnp.minimum(jnp.maximum(gap, -1.0), 1.0)
                    mat[c, rows, js] = (sign * apart).astype(BF16)
            return carry

        lax.fori_loop(0, KP // MB, build, 0)

        def arrive(k, carry):
            source = lax.rem(leaf + k, PEERS)
            pltpu.make_async_remote_copy(
                src_ref=yz.at[0],
                dst_ref=recv_z.at[source],
                send_sem=z_send.at[0],
                recv_sem=z_recv.at[source],
                device_id=(line, source),
                device_id_type=MESH,
            ).wait_recv()
            pltpu.make_async_remote_copy(
                src_ref=yw.at[0],
                dst_ref=recv_w.at[source],
                send_sem=w_send.at[0],
                recv_sem=w_recv.at[source],
                device_id=(line, source),
                device_id_type=MESH,
            ).wait_recv()
            return carry

        lax.fori_loop(1, PEERS, arrive, 0)

        def unpack(i, carry):
            z_sum, w_sum = carry
            rows = pl.ds(pl.multiple_of(i * MB, MB), MB)
            chunk = pl.ds(i * (MB // HP), MB // HP)
            v = col[2, rows]
            z = recv_z[chunk].reshape(MB, 128).astype(F32) * v
            ws = recv_w[chunk, 0].reshape(MB, 128).astype(jnp.int32).astype(F32) * v
            wf = recv_w[chunk, 1].reshape(MB, 128).astype(jnp.int32).astype(F32) * v
            s_high = jnp.floor(ws * (1.0 / 256.0))
            s_low = ws - 256.0 * s_high
            f_high = jnp.floor(wf * (1.0 / 256.0))
            f_low = wf - 256.0 * f_high
            x[rows, 0:128] = z.astype(BF16)
            x[rows, 128:256] = f_high.astype(BF16)
            x[rows, 256:384] = f_low.astype(BF16)
            x[rows, 384:512] = jnp.where(low, s_high, roll_half(s_low)).astype(BF16)
            x[rows, 512:640] = jnp.where(low, roll_half(s_high), s_low).astype(BF16)
            return (
                z_sum + jnp.sum(z, axis=0, keepdims=True),
                w_sum + jnp.sum(ws + jnp.abs(wf), axis=0, keepdims=True),
            )

        empty = jnp.zeros((1, 128), F32)
        z_sum, w_sum = lax.fori_loop(0, KP // MB, unpack, (empty, empty))
        unit = ONE_TOP / CODE
        z_power = jnp.floor(jnp.log2(jnp.maximum(z_sum, 1e-30))) + 1.0
        w_power = jnp.floor(jnp.log2(jnp.maximum(w_sum * unit, 1e-30))) + 1.0
        z_scale = CODE * jnp.exp2(-z_power)
        w_scale = (CODE * unit) * jnp.exp2(-w_power)
        pad = lax.rem(lax.broadcasted_iota(jnp.int32, (MB, 128), 0), HP) >= hands
        low_part = jnp.where(low, 256.0, 1.0)

        def block(k, carry):
            i = lax.rem(leaf // 8 + k, KP // MB)
            rows = pl.ds(pl.multiple_of(i * MB, MB), MB)
            d = jnp.dot(mat[2, rows], x[:, 0:384], preferred_element_type=F32)
            s0z = jnp.dot(mat[0, rows], x[:, 0:128], preferred_element_type=F32)
            s0w = jnp.dot(mat[0, rows], x[:, 384:512], preferred_element_type=F32)
            s1z = jnp.dot(mat[1, rows], x[:, 0:128], preferred_element_type=F32)
            s1w = jnp.dot(mat[1, rows], x[:, 512:640], preferred_element_type=F32)
            v = col[2, rows]
            s0w = s0w * low_part
            s1w = s1w * low_part
            s0w = s0w + roll_half(s0w)
            s1w = s1w + roll_half(s1w)
            act = jnp.where(low, s0w, s1w) + 256.0 * d[:, 128:256] + d[:, 256:384]
            tiles = (
                (act * (v * w_scale), w_power),
                (jnp.where(low, s0z, s1z) * (v * z_scale), z_power),
                (d[:, 0:128] * (v * z_scale), z_power),
            )
            for j, (value, power) in enumerate(tiles):
                value = jnp.minimum(jnp.maximum(nearest(value), -32767.0), 32767.0)
                coded = code(jnp.where(pad, power, value))
                out[pl.ds(i * (MB // HP), MB // HP), j] = coded.reshape(MB // HP, HP, 128)

            def send(m, carry):
                peer = i * (MB // HP) + m

                @pl.when(peer != leaf)
                def _():
                    out_copy(peer).start()

                @pl.when(peer == leaf)
                def _():
                    back[w_self] = out[peer]

                return carry

            lax.fori_loop(0, MB // HP, send, 0)
            return carry

        lax.fori_loop(0, KP // MB, block, 0)

    def collect(k, carry):
        w = lax.rem(first_worker + k, WORKERS)
        peer = worker_leaf(w)

        @pl.when(peer != leaf)
        def _():
            pltpu.make_async_remote_copy(
                src_ref=out.at[0],
                dst_ref=back.at[w],
                send_sem=out_send.at[0],
                recv_sem=out_recv.at[w],
                device_id=(line, peer),
                device_id_type=MESH,
            ).wait_recv()
            z_copy(w, peer).wait_send()
            w_copy(w, peer).wait_send()

        return carry

    lax.fori_loop(0, WORKERS, collect, 0)

    @pl.when(is_worker)
    def _():
        def sent(k, carry):
            out_copy(lax.rem(leaf + k, PEERS)).wait_send()
            return carry

        lax.fori_loop(1, PEERS, sent, 0)

    def turn_sent(k, carry):
        turn_copy(lax.rem(line + k, lines), line).wait_send()
        return carry

    lax.fori_loop(1, lines, turn_sent, 0)


PER_STEP = 4


def update_kernel(rz, ro, back, pots, kinds, new_rz, new_ro, lines, sums):
    hands = rz.shape[0]
    lane = lanes(hands)
    show, fold = leaf_scales(pots, kinds, hands)
    i = pl.program_id(0)

    @pl.when(i == 0)
    def _():
        sums[...] = jnp.zeros_like(sums)

    sum_zero, sum_one = sums[0], sums[1]
    for w in range(PER_STEP):
        r, zs = zero_shares(rz, w, lane)
        regrets, os = one_shares(ro, w, lane)
        values = []
        for j in range(3):
            coded = back[w, j].astype(jnp.int32).astype(F32)
            scale = jnp.exp2(coded[hands : hands + 1]) * (1.0 / CODE)
            values.append(coded[0:hands] * scale)
        act, sz, dz = values
        node = action_sum(zs * act, lane)
        new_rz[:, pl.ds(128 * w, 128)] = jnp.maximum(r + act - node, 0.0)
        leaf_one = [show[b] * sz - fold[b] * dz for b in range(MOVES_ONE)]
        node_one = os[0] * leaf_one[0] + os[1] * leaf_one[1] + os[2] * leaf_one[2]
        new = [jnp.maximum(regrets[b] + leaf_one[b] - node_one, 0.0) for b in range(MOVES_ONE)]
        native = join_moves(new, lane)
        for v in range(3):
            new_ro[:, pl.ds(384 * w + 128 * v, 128)] = native[v]
        sum_zero = sum_zero + node
        sum_one = sum_one + node_one
    sums[0] = sum_zero
    sums[1] = sum_one

    @pl.when(i == pl.num_programs(0) - 1)
    def _():
        node_once = jnp.where(lane % 64 < SUBGAMES, sum_zero, 0.0)
        for k, total in enumerate((node_once, sum_one)):
            lines[k] = CHANCE * lax.dot_general(
                tile_selector(),
                total,
                (((1,), (1,)), ((), ())),
                precision=lax.Precision.HIGHEST,
                preferred_element_type=F32,
            )


def root_kernel(values, turn_regret, turn_total, new_turn, roots, own, parts, send_sem, recv_sem):
    line, leaf = lax.axis_index("river"), lax.axis_index("leaf")
    lines = parts.shape[0]
    barrier = pltpu.get_barrier_semaphore()

    def greet(k, carry):
        peer = lax.rem(line + k, lines)
        pl.semaphore_signal(barrier, inc=1, device_id=(peer, leaf), device_id_type=MESH)
        return carry

    lax.fori_loop(1, lines, greet, 0)
    own[0] = (turn_regret[...] / turn_total[...]) * values[0]
    own[1] = values[1]
    pl.semaphore_wait(barrier, lines - 1)

    def copy(peer, slot):
        return pltpu.make_async_remote_copy(
            src_ref=own,
            dst_ref=parts.at[slot],
            send_sem=send_sem.at[peer],
            recv_sem=recv_sem.at[slot],
            device_id=(peer, leaf),
            device_id_type=MESH,
        )

    def start(k, carry):
        copy(lax.rem(line + k, lines), line).start()
        return carry

    lax.fori_loop(1, lines, start, 0)
    parts[line] = own[...]

    def wait(k, carry):
        peer = lax.rem(line + k, lines)
        copy(peer, peer).wait_recv()
        copy(peer, line).wait_send()
        return carry

    lax.fori_loop(1, lines, wait, 0)
    total = parts[0]
    for t in range(1, lines):
        total = total + parts[t]
    roots[...] = total
    new_turn[...] = jnp.maximum(turn_regret[...] + values[0] - total[0], 0.0)


VM = pl.BlockSpec(memory_space=pltpu.VMEM)
SM = pl.BlockSpec(memory_space=pltpu.SMEM)
HB = pl.BlockSpec(memory_space=pl.ANY)
LIMIT = 56 << 20


def local(
    range_zero,
    range_one,
    turn_regret,
    river_regret_zero,
    river_regret_one,
    hand_cards,
    dealt_cards,
    hand_ranks,
    leaf_pots,
    leaf_kinds,
):
    hands = range_zero.shape[1]
    lines = lax.axis_size("river")
    rz = river_regret_zero[0]
    ro = river_regret_one[0]
    tr = turn_regret[0]
    cards = jnp.pad(
        hand_cards.T.reshape(2, PEERS, hands), ((0, 0), (0, 0), (0, HP - hands)), constant_values=52
    ).reshape(2, KP)
    cards = jnp.pad(cards.astype(F32), ((0, 6), (0, 0)))
    _, w_self = leaf_worker(lax.axis_index("leaf"))
    w_self = jnp.minimum(w_self, WORKERS - 1)
    ranks = lax.dynamic_slice_in_dim(hand_ranks, 2 * w_self, 2, 0)
    ranks = jnp.pad(ranks.reshape(2, PEERS, hands), ((0, 0), (0, 0), (0, HP - hands))).reshape(2, KP)
    ranks = jnp.pad(ranks.astype(F32), ((0, 6), (0, 0)))
    dma = pltpu.SemaphoreType.DMA
    back, turn_total = pl.pallas_call(
        lead_kernel,
        out_shape=(
            jax.ShapeDtypeStruct((WORKERS, 3, HP, 128), jnp.int16),
            jax.ShapeDtypeStruct(tr.shape, F32),
        ),
        in_specs=[HB, HB, VM, VM, VM, VM, VM, SM, SM, SM],
        out_specs=(VM, VM),
        scratch_shapes=[
            pltpu.VMEM(rz.shape, F32),
            pltpu.VMEM(ro.shape, F32),
            pltpu.VMEM((lines,) + tr.shape, F32),
            pltpu.VMEM((WORKERS, HP, 128), BF16),
            pltpu.VMEM((WORKERS, 2, HP, 128), jnp.int16),
            pltpu.VMEM((PEERS, HP, 128), BF16),
            pltpu.VMEM((PEERS, 2, HP, 128), jnp.int16),
            pltpu.VMEM((KP, 640), BF16),
            pltpu.VMEM((3, KP, KP), BF16),
            pltpu.VMEM((3, KP, 128), F32),
            pltpu.VMEM((KP, 128), BF16),
            pltpu.VMEM((PEERS, 3, HP, 128), jnp.int16),
            dma((2,)),
            dma((lines,)),
            dma((lines,)),
            dma((WORKERS,)),
            dma((PEERS,)),
            dma((WORKERS,)),
            dma((PEERS,)),
            dma((PEERS,)),
            dma((WORKERS,)),
        ],
        compiler_params=pltpu.CompilerParams(
            collective_id=1, has_side_effects=True, vmem_limit_bytes=LIMIT
        ),
    )(rz, ro, range_zero, range_one, tr, cards, ranks, dealt_cards, leaf_pots, leaf_kinds)
    steps = WORKERS // PER_STEP
    new_rz, new_ro, values = pl.pallas_call(
        update_kernel,
        grid=(steps,),
        out_shape=(
            jax.ShapeDtypeStruct(rz.shape, F32),
            jax.ShapeDtypeStruct(ro.shape, F32),
            jax.ShapeDtypeStruct((2,) + tr.shape, F32),
        ),
        in_specs=[
            pl.BlockSpec((hands, 128 * PER_STEP), lambda i: (0, i)),
            pl.BlockSpec((hands, 384 * PER_STEP), lambda i: (0, i)),
            pl.BlockSpec((PER_STEP, 3, HP, 128), lambda i: (i, 0, 0, 0)),
            SM,
            SM,
        ],
        out_specs=(
            pl.BlockSpec((hands, 128 * PER_STEP), lambda i: (0, i)),
            pl.BlockSpec((hands, 384 * PER_STEP), lambda i: (0, i)),
            pl.BlockSpec((2,) + tr.shape, lambda i: (0, 0, 0)),
        ),
        scratch_shapes=[pltpu.VMEM((2, hands, 128), F32)],
        compiler_params=pltpu.CompilerParams(vmem_limit_bytes=16 << 20),
    )(rz, ro, back, leaf_pots, leaf_kinds)
    new_turn, roots = pl.pallas_call(
        root_kernel,
        out_shape=(
            jax.ShapeDtypeStruct(tr.shape, F32),
            jax.ShapeDtypeStruct((2,) + tr.shape, F32),
        ),
        in_specs=[VM, VM, VM],
        out_specs=(VM, VM),
        scratch_shapes=[
            pltpu.VMEM((2,) + tr.shape, F32),
            pltpu.VMEM((lines, 2) + tr.shape, F32),
            dma((lines,)),
            dma((lines,)),
        ],
        compiler_params=pltpu.CompilerParams(collective_id=2, has_side_effects=True),
    )(values, tr, turn_total)
    return (new_turn[None], new_rz[None], new_ro[None], roots)


def solution(mesh):
    placed = (
        P(None, "leaf"),
        P(None, "leaf"),
        P("river", None, "leaf"),
        P("river", "leaf", None),
        P("river", "leaf", None),
        P(),
        P(),
        P(),
        P("river", None),
        P("river", None),
    )
    return jax.shard_map(
        local,
        mesh=mesh,
        in_specs=placed,
        out_specs=(
            P("river", None, "leaf"),
            P("river", "leaf", None),
            P("river", "leaf", None),
            P(None, None, "leaf"),
        ),
        check_vma=False,
    )
```

time: 175 us -> 102 us (0.58)
  the two profiles are of different devices: /device:TPU:6 before, /device:TPU:38 now
where the time goes in v2:
time: 102 us
  Pallas kernels  87.2 us (85%)
  local copies, waits for them, and re-layouts  13.8 us (14%)
    pallas_call x1, Pallas kernels, local(): pl.pallas_call(lead_kernel, out_shape=(jax.ShapeDtypeStruct((WORKERS, 3,...  74.1 us
    unnamed x26, local copies, waits for them, and re-layouts  11.4 us
    pallas_call x1, Pallas kernels, local(): pl.pallas_call(root_kernel, out_shape=(jax.ShapeDtypeStruct(tr.shape, F32...  7.25 us
    pallas_call x1, Pallas kernels, local(): pl.pallas_call(update_kernel, grid=(steps,), out_shape=(jax.ShapeDtypeStr...  5.89 us

profile of v2, /device:TPU:38, one launch (start us, length us, event | category | flops | bytes accessed | tf_op | source)
XLA Modules:
  0.0 101.8 jit_solution(16857392898606728103)
XLA Ops:
  0.6 0.0 copy-start
  0.6 0.0 copy-start.7
  0.7 0.9 copy-done
  1.6 0.1 reshape.19
  1.7 0.1 convert_element_type.18
  1.8 0.8 reshape.18
  2.6 0.1 convert_element_type.16
  2.7 0.6 pad.15.cards
  3.4 0.6 pad.17.ranks
  4.0 2.0 %copy.21 = f32[1,42,3072]{2,1,0:T(8,128)} copy(f32[1,42,3072]{2,0,1:T(1,128)} %param.13) | data formatting | bytes 1032192
  5.9 0.0 copy-done.7
  5.9 1.5 %copy.20 = f32[1,42,9216]{2,1,0:T(8,128)} copy(f32[1,42,9216]{2,0,1:T(1,128)S(1)} %copy-done.7) | data formatting | bytes 3096576
  7.5 0.0 copy-start.1
  7.5 0.0 copy-start.2
  7.5 0.0 copy-start.5
  7.5 0.0 copy-start.6
  7.5 74.1 %shard_map.129 = (s16[24,3,48,128]{3,2,1,0:T(8,128)(2,1)}, f32[16,42]{1,0:T(8,128)}) custom-call(f32[42,3072]{1,0:T(8,128)} %bitcast.13, f32[42,9216]{1,0:T(8,128)} %bitcast.11, f32[16,42]{1,0:T(8,128)} %range_zero.1, f32[16,42]{1,0:T(8,128)} %range_one.1, f32[16,42]{1,0:T(8,128)} %bitcast.17, f32[8,1536]{1,0:T(8,128)} %pad.15.cards, f32[8,1536]{1,0:T(8,128)} %pad.17.ranks, ...), custom_call_target="tpu_custom_call" | custom-call | tf_op jit(solution)/shard_map/pallas_call | solution.py:600
  81.6 0.0 copy-done.1
  81.6 0.0 copy-done.2
  81.6 0.0 copy-done.5
  81.6 0.0 copy-done.6
  81.6 0.0 copy-start.3
  81.6 1.2 %copy-done.3 = s16[24,3,48,128]{3,2,1,0:T(8,128)(2,1)S(1)} copy-done((s16[24,3,48,128]{3,2,1,0:T(8,128)(2,1)S(1)}, s16[24,3,48,128]{3,2,1,0:T(8,128)(2,1)}, u32[]{:S(2)}) %copy-start.3) | copy-done | bytes 884760
  82.8 5.9 %shard_map.130 = (f32[42,3072]{1,0:T(8,128)S(1)}, f32[42,9216]{1,0:T(8,128)S(1)}, f32[2,16,42]{2,1,0:T(8,128)S(1)}) custom-call(f32[42,3072]{1,0:T(8,128)S(1)} %bitcast.14, f32[42,9216]{1,0:T(8,128)S(1)} %bitcast.12, s16[24,3,48,128]{3,2,1,0:T(8,128)(2,1)S(1)} %copy-done.3, s32[1,12]{1,0:T(1,128)S(1)} %copy-done.5, s32[1,12]{1,0:T(1,128)S(1)} %copy-done.6), custom_call_target="tpu_custom_call" | custom-call | tf_op jit(solution)/shard_map/pallas_call | solution.py:636
  88.7 0.0 copy-start.4
  88.7 0.6 copy-done.4
  89.3 1.3 %copy.14 = f32[1,42,3072]{2,0,1:T(1,128)} copy(f32[1,42,3072]{2,1,0:T(8,128)S(1)} %bitcast.16) | data formatting | bytes 1032192
  90.6 7.3 %shard_map.131 = (f32[16,42]{1,0:T(8,128)}, f32[2,16,42]{2,1,0:T(8,128)}) custom-call(f32[2,16,42]{2,1,0:T(8,128)} %copy-done.4, f32[16,42]{1,0:T(8,128)} %bitcast.18, f32[16,42]{1,0:T(8,128)} %get-tuple-element.13.turn_total), custom_call_target="tpu_custom_call" | custom-call | tf_op jit(solution)/shard_map/pallas_call | solution.py:659
  97.9 0.0 copy-start.9
  97.9 0.0 copy-start.8
  97.9 2.7 %copy.15 = f32[1,42,9216]{2,0,1:T(1,128)} copy(f32[1,42,9216]{2,1,0:T(8,128)S(1)} %bitcast.15) | data formatting | bytes 3096576
  100.6 0.0 copy-done.9
  100.6 0.6 copy.24
  101.2 0.0 copy-done.8
  101.2 0.6 copy.25
  (3 shorter events, 0.0 us)
Async XLA Ops:
  0.6 1.0 copy-start
  0.6 5.3 %copy-start.7 = (f32[1,42,9216]{2,0,1:T(1,128)S(1)}, f32[1,42,9216]{2,0,1:T(1,128)}, u32[]{:S(2)}) copy-start(f32[1,42,9216]{2,0,1:T(1,128)} %param.14) | copy-start | bytes 4644868
  7.5 74.1 %copy-start.1 = (f32[1,42,9216]{2,1,0:T(8,128)S(1)}, f32[1,42,9216]{2,1,0:T(8,128)}, u32[]{:S(2)}) copy-start(f32[1,42,9216]{2,1,0:T(8,128)} %copy.20) | copy-start | bytes 4644868
  7.5 74.1 %copy-start.2 = (f32[1,42,3072]{2,1,0:T(8,128)S(1)}, f32[1,42,3072]{2,1,0:T(8,128)}, u32[]{:S(2)}) copy-start(f32[1,42,3072]{2,1,0:T(8,128)} %copy.21) | copy-start | bytes 1548292
  7.5 74.1 %copy-start.5 = (s32[1,12]{1,0:T(1,128)S(1)}, s32[1,12]{1,0:T(1,128)}, u32[]{:S(2)}) copy-start(s32[1,12]{1,0:T(1,128)} %pots.3) | copy-start | bytes 148
  7.5 74.1 %copy-start.6 = (s32[1,12]{1,0:T(1,128)S(1)}, s32[1,12]{1,0:T(1,128)}, u32[]{:S(2)}) copy-start(s32[1,12]{1,0:T(1,128)} %kinds.3) | copy-start | bytes 148
  81.6 1.2 %copy-start.3 = (s16[24,3,48,128]{3,2,1,0:T(8,128)(2,1)S(1)}, s16[24,3,48,128]{3,2,1,0:T(8,128)(2,1)}, u32[]{:S(2)}) copy-start(s16[24,3,48,128]{3,2,1,0:T(8,128)(2,1)} %get-tuple-element.11.back) | copy-start | bytes 2654212
  88.7 0.6 copy-start.4
  97.9 2.7 %copy-start.9 = (f32[16,42]{1,0:T(8,128)S(1)}, f32[16,42]{1,0:T(8,128)}, u32[]{:S(2)}) copy-start(f32[16,42]{1,0:T(8,128)} %get-tuple-element.14) | copy-start | bytes 8068
  97.9 3.3 %copy-start.8 = (f32[2,16,42]{2,1,0:T(8,128)S(1)}, f32[2,16,42]{2,1,0:T(8,128)}, u32[]{:S(2)}) copy-start(f32[2,16,42]{2,1,0:T(8,128)} %get-tuple-element.29) | copy-start | bytes 16132

commit v3 on v2

v3 whole, which is shorter than its diff:
```python
import jax
import jax.numpy as jnp
from jax import lax
from jax.experimental import pallas as pl
from jax.experimental.pallas import tpu as pltpu
from jax.sharding import PartitionSpec as P

MESH = pl.DeviceIdType.MESH
F32 = jnp.float32
BF16 = jnp.bfloat16
RIVERS = 48
MOVES_ZERO = 4
MOVES_ONE = 3
SUBGAMES = 16
WORKERS = 24
PEERS = 32
HP = 48
KP = PEERS * HP
MB = 384
BLOCK = 384
CHANCE = 1.0 / 44.0


def worker_leaf(w):
    z = w // 3
    x = lax.rem(w - 3 * z + 1 + z, 4)
    return 4 * z + x


def leaf_worker(leaf):
    z = leaf // 4
    x = leaf - 4 * z
    k = lax.rem(x - 1 - z + 12, 4)
    return k, 3 * z + k


def lanes(rows):
    return lax.broadcasted_iota(jnp.int32, (rows, 128), 1)


def gather_lanes(x, index):
    return jnp.take_along_axis(x, index, axis=1, mode="promise_in_bounds")


def roll_half(x):
    return pltpu.roll(x, 64, 1)


def action_sum(x, lane):
    x = x + gather_lanes(x, (lane & 64) | ((lane + 16) & 63))
    return x + gather_lanes(x, (lane & 64) | ((lane + 32) & 63))


def split_moves(tiles, lane):
    slot, sub = lane // 16, lane % 16
    out = []
    for b in range(MOVES_ONE):
        group = (3 * (slot - b + 8)) % 8
        tile = (3 * group + b) // 8
        picked = jnp.where(tile == 0, tiles[0], jnp.where(tile == 1, tiles[1], tiles[2]))
        out.append(gather_lanes(picked, ((3 * slot + b) % 8) * 16 + sub))
    return out


def join_moves(parts, lane):
    slot, sub = lane // 16, lane % 16
    moved = []
    for b in range(MOVES_ONE):
        group = (3 * (slot - b + 8)) % 8
        moved.append(gather_lanes(parts[b], group * 16 + sub))
    out = []
    for v in range(3):
        b = (8 * v + slot) % 3
        out.append(jnp.where(b == 0, moved[0], jnp.where(b == 1, moved[1], moved[2])))
    return out


def tile_selector():
    sub = lax.broadcasted_iota(jnp.int32, (SUBGAMES, 128), 0)
    lane = lanes(SUBGAMES)
    return (lane % SUBGAMES == sub).astype(F32)


def to_lanes(x):
    return lax.dot_general(
        x,
        tile_selector(),
        (((0,), (0,)), ((), ())),
        precision=lax.Precision.HIGHEST,
        preferred_element_type=F32,
    )


def leaf_scales(pots, kinds, rows):
    action = (lanes(rows) // SUBGAMES) % MOVES_ZERO
    show, fold = [], []
    for b in range(MOVES_ONE):
        s = jnp.zeros((rows, 128), F32)
        f = jnp.zeros((rows, 128), F32)
        for a in range(MOVES_ZERO):
            pot = pots[0, a * MOVES_ONE + b].astype(F32)
            kind = kinds[0, a * MOVES_ONE + b]
            here = action == a
            s = jnp.where(here, jnp.where(kind == 0, pot, 0.0), s)
            f = jnp.where(here, jnp.where(kind == 0, 0.0, jnp.where(kind == 1, pot, -pot)), f)
        show.append(s)
        fold.append(f)
    return show, fold


ONE_TOP = 64.0 * 0.001 * 1.005
CODE = 32760.0
ROWS = 128
STAGE = 136


def column(rows, select):
    return lax.dot_general(
        rows, select, (((0,), (0,)), ((), ())), preferred_element_type=F32
    )


def code(x):
    return x.astype(jnp.int32).astype(jnp.int16)


def decode(x):
    return x.astype(jnp.int32).astype(F32)


def nearest(x):
    return jnp.floor(x + 0.5)


def power_above(x):
    return jnp.floor(jnp.log2(jnp.maximum(x, 1e-30))) + 1.0


def zero_shares(rz, w, lane, hands):
    x = rz[pl.ds(w, hands, stride=WORKERS)]
    return x, x / action_sum(x, lane)


def one_shares(ro, w, lane, hands):
    tiles = [ro[pl.ds(3 * w + v, hands, stride=3 * WORKERS)] for v in range(3)]
    regrets = split_moves(tiles, lane)
    scale = 1.0 / (regrets[0] + regrets[1] + regrets[2])
    return regrets, [r * scale for r in regrets]


def kernel(
    rz_hbm,
    ro_hbm,
    range_zero,
    range_one,
    turn_regret,
    cards,
    all_ranks,
    dealt,
    pots,
    kinds,
    new_turn,
    new_rz,
    new_ro,
    roots,
    rz,
    ro,
    turns,
    yq,
    recv,
    stage,
    spread,
    card_pad,
    rank_row,
    x,
    mat,
    col,
    inc,
    out,
    back,
    own,
    parts,
    load_sem,
    turn_send,
    turn_recv,
    y_send,
    y_recv,
    out_send,
    out_recv,
    root_send,
    root_recv,
):
    line, leaf = lax.axis_index("river"), lax.axis_index("leaf")
    lines = turns.shape[0]
    k_self, w_self = leaf_worker(leaf)
    is_worker = k_self < 3
    hands = turn_regret.shape[1]
    first_worker = 3 * (leaf // 4)

    loads = [
        pltpu.make_async_copy(rz_hbm, rz, load_sem.at[0]),
        pltpu.make_async_copy(ro_hbm, ro, load_sem.at[1]),
    ]
    for load in loads:
        load.start()

    barrier = pltpu.get_barrier_semaphore()

    def greet_leaf(k, carry):
        peer = lax.rem(leaf + k, PEERS)
        pl.semaphore_signal(barrier, inc=1, device_id=(line, peer), device_id_type=MESH)
        return carry

    def greet_line(k, carry):
        peer = lax.rem(line + k, lines)
        pl.semaphore_signal(barrier, inc=1, device_id=(peer, leaf), device_id_type=MESH)
        return carry

    lax.fori_loop(1, lines, greet_line, 0)
    lax.fori_loop(1, PEERS, greet_leaf, 0)

    lane = lanes(hands)
    weight_one = to_lanes(range_one[...])
    show, fold = leaf_scales(pots, kinds, 8)
    show = [s[0:1] for s in show]
    fold = [f[0:1] for f in fold]
    unit = CODE / ONE_TOP
    stage[...] = jnp.zeros_like(stage)
    for load in loads:
        load.wait()
    pl.semaphore_wait(barrier, PEERS - 1 + lines - 1)

    def line_copy(src, dst, sends, recvs, peer, slot):
        return pltpu.make_async_remote_copy(
            src_ref=src,
            dst_ref=dst.at[slot],
            send_sem=sends.at[peer],
            recv_sem=recvs.at[slot],
            device_id=(peer, leaf),
            device_id_type=MESH,
        )

    def line_sum(src, dst, sends, recvs):
        def start(k, carry):
            line_copy(src, dst, sends, recvs, lax.rem(line + k, lines), line).start()
            return carry

        lax.fori_loop(1, lines, start, 0)
        dst[line] = src[...]

        def wait(k, carry):
            peer = lax.rem(line + k, lines)
            line_copy(src, dst, sends, recvs, peer, peer).wait_recv()
            return carry

        lax.fori_loop(1, lines, wait, 0)
        total = dst[0]
        for t in range(1, lines):
            total = total + dst[t]
        return total

    def line_sent(src, dst, sends, recvs):
        def wait(k, carry):
            line_copy(src, dst, sends, recvs, lax.rem(line + k, lines), line).wait_send()
            return carry

        lax.fori_loop(1, lines, wait, 0)

    turn_share = turn_regret[...] / line_sum(turn_regret, turns, turn_send, turn_recv)
    weight_zero = to_lanes(range_zero[...] * turn_share)

    def y_copy(w, peer):
        return pltpu.make_async_remote_copy(
            src_ref=yq.at[w],
            dst_ref=recv.at[leaf],
            send_sem=y_send.at[w],
            recv_sem=y_recv.at[leaf],
            device_id=(line, peer),
            device_id_type=MESH,
        )

    def prepare(k, carry):
        w = lax.rem(first_worker + k, WORKERS)
        slot = lax.rem(k, 2)
        _, zs = zero_shares(rz, w, lane, hands)
        _, os = one_shares(ro, w, lane, hands)
        z = (weight_zero * zs).astype(BF16).astype(F32)
        power = power_above(jnp.max(z, axis=0, keepdims=True))
        o = [(weight_one * s).astype(BF16).astype(F32) for s in os]
        stage[slot, 0:hands] = nearest(z * (CODE * jnp.exp2(-power)))
        for j, scale in enumerate((show, fold)):
            mixed = o[0] * scale[0] + o[1] * scale[1] + o[2] * scale[2]
            stage[slot, (j + 1) * hands : (j + 2) * hands] = nearest(mixed * unit)
        stage[slot, 3 * hands : 3 * hands + 1] = power
        yq[w] = code(stage[slot, 0:ROWS])
        peer = worker_leaf(w)

        @pl.when(peer != leaf)
        def _():
            y_copy(w, peer).start()

        @pl.when(peer == leaf)
        def _():
            recv[leaf] = yq[w]

        return carry

    lax.fori_loop(0, WORKERS, prepare, 0)

    def out_copy(peer):
        return pltpu.make_async_remote_copy(
            src_ref=out.at[peer],
            dst_ref=back.at[w_self],
            send_sem=out_send.at[peer],
            recv_sem=out_recv.at[w_self],
            device_id=(line, peer),
            device_id_type=MESH,
        )

    @pl.when(is_worker)
    def _():
        low = lanes(8)[0:1] < 64
        source_hand = lax.broadcasted_iota(jnp.int32, (PEERS * hands, 128), 0)
        place = source_hand + (HP - hands) * (source_hand // hands)
        for j in range(KP // 128):
            here = lanes(PEERS * hands) + 128 * j
            spread[:, pl.ds(128 * j, 128)] = (place == here).astype(F32).astype(BF16)
        card_pad[...] = jnp.zeros_like(card_pad)
        card_pad[0:2] = (cards[...] + 1).astype(F32)
        eight = pl.ds(pl.multiple_of(8 * (w_self // 4), 8), 8)
        ranks = all_ranks[eight].astype(F32)
        high = jnp.floor(ranks * (1.0 / 64.0))
        rest = ranks - 64.0 * high

        def spread_rows(v):
            return jnp.dot(v.astype(BF16), spread[...], preferred_element_type=F32)

        card_rows = spread_rows(card_pad[...]).astype(BF16)
        high_rows = spread_rows(high)
        rest_rows = spread_rows(rest)
        one_row = lax.broadcasted_iota(jnp.int32, (8, 128), 0)
        pick = lambda r, scale: jnp.where(one_row == r, scale, 0.0).astype(BF16)
        first = column(card_rows, pick(0, 1.0)) - 1.0
        second = column(card_rows, pick(1, 1.0)) - 1.0
        usable = (first < 52.0) & (second < 52.0) & (first >= 0.0)
        for k in range(4):
            board = dealt[k].astype(F32)
            usable = usable & (first != board) & (second != board)
        rivers = [dealt[4 + 2 * w_self + c].astype(F32) for c in range(2)]
        river = jnp.where(low, rivers[0], rivers[1])
        col[2] = (usable & (first != river) & (second != river)).astype(F32)
        card = lanes(KP).astype(F32)
        inc[...] = ((first == card) | (second == card)).astype(F32).astype(BF16)
        rank_rows = 64.0 * high_rows + rest_rows
        wide_row = lax.broadcasted_iota(jnp.int32, (8, KP), 0)
        for c in range(2):
            r = 2 * lax.rem(w_self, 4) + c
            rank_row[c : c + 1] = jnp.sum(
                jnp.where(wide_row == r, rank_rows, 0.0), axis=0, keepdims=True
            )
            col[c] = column(high_rows.astype(BF16), pick(r, 64.0)) + column(
                rest_rows.astype(BF16), pick(r, 1.0)
            )

        def build(i, carry):
            rows = pl.ds(pl.multiple_of(i * MB, MB), MB)
            for j in range(KP // 128):
                js = pl.ds(128 * j, 128)
                shared = lax.dot_general(
                    inc[rows], inc[js], (((1,), (1,)), ((), ())), preferred_element_type=F32
                )
                apart = jnp.maximum(1.0 - shared, 0.0)
                mat[2, rows, js] = apart.astype(BF16)
                for c in range(2):
                    gap = col[c, rows] - rank_row[c : c + 1, js]
                    sign = jnp.minimum(jnp.maximum(gap, -1.0), 1.0)
                    mat[c, rows, js] = (sign * apart).astype(BF16)
            return carry

        lax.fori_loop(0, KP // MB, build, 0)

        def arrive(k, carry):
            z_sum, w_sum = carry
            source = lax.rem(leaf + k, PEERS)
            slot = lax.rem(k, 2)

            @pl.when(k > 0)
            def _():
                pltpu.make_async_remote_copy(
                    src_ref=yq.at[0],
                    dst_ref=recv.at[source],
                    send_sem=y_send.at[0],
                    recv_sem=y_recv.at[source],
                    device_id=(line, source),
                    device_id_type=MESH,
                ).wait_recv()

            rows = pl.ds(pl.multiple_of(source * HP, HP), HP)
            v = col[2, rows]
            coded = decode(recv[source])
            stage[slot, 0:ROWS] = coded
            scale = jnp.exp2(stage[slot, 3 * hands : 3 * hands + 1]) * (1.0 / CODE)
            z = (stage[slot, 0:HP] * (v * scale)).astype(BF16)
            ws = stage[slot, hands : hands + HP] * v
            wf = stage[slot, 2 * hands : 2 * hands + HP] * v
            s_high = jnp.floor(ws * (1.0 / 256.0))
            s_low = ws - 256.0 * s_high
            f_high = jnp.floor(wf * (1.0 / 256.0))
            f_low = wf - 256.0 * f_high
            x[rows, 0:128] = z
            x[rows, 128:256] = f_high.astype(BF16)
            x[rows, 256:384] = f_low.astype(BF16)
            x[rows, 384:512] = jnp.where(low, s_high, roll_half(s_low)).astype(BF16)
            x[rows, 512:640] = jnp.where(low, roll_half(s_high), s_low).astype(BF16)
            return (z_sum + z.astype(F32), w_sum + ws + jnp.abs(wf))

        empty = jnp.zeros((HP, 128), F32)
        z_sum, w_sum = lax.fori_loop(0, PEERS, arrive, (empty, empty))
        z_power = power_above(jnp.sum(z_sum, axis=0, keepdims=True))
        w_power = power_above(jnp.sum(w_sum, axis=0, keepdims=True) * (1.0 / unit))
        z_scale = CODE * jnp.exp2(-z_power)
        w_scale = (CODE / unit) * jnp.exp2(-w_power)
        low_part = jnp.where(low, 256.0, 1.0)

        def block(k, carry):
            i = lax.rem(leaf // (BLOCK // HP) + k, KP // BLOCK)
            rows = pl.ds(pl.multiple_of(i * BLOCK, BLOCK), BLOCK)
            d = jnp.dot(mat[2, rows], x[:, 0:384], preferred_element_type=F32)
            s0z = jnp.dot(mat[0, rows], x[:, 0:128], preferred_element_type=F32)
            s0w = jnp.dot(mat[0, rows], x[:, 384:512], preferred_element_type=F32)
            s1z = jnp.dot(mat[1, rows], x[:, 0:128], preferred_element_type=F32)
            s1w = jnp.dot(mat[1, rows], x[:, 512:640], preferred_element_type=F32)
            v = col[2, rows]
            s0w = s0w * low_part
            s1w = s1w * low_part
            s0w = s0w + roll_half(s0w)
            s1w = s1w + roll_half(s1w)
            act = jnp.where(low, s0w, s1w) + 256.0 * d[:, 128:256] + d[:, 256:384]
            tiles = (
                act * (v * w_scale),
                jnp.where(low, s0z, s1z) * (v * z_scale),
                d[:, 0:128] * (v * z_scale),
            )
            tiles = [nearest(jnp.minimum(jnp.maximum(t, -CODE), CODE)) for t in tiles]
            for m in range(BLOCK // HP):
                for j in range(3):
                    stage[m, j * hands : j * hands + HP] = tiles[j][m * HP : (m + 1) * HP]
                stage[m, 3 * hands : 3 * hands + 1] = w_power
                stage[m, 3 * hands + 1 : 3 * hands + 2] = z_power
                peer = i * (BLOCK // HP) + m
                out[peer] = code(stage[m, 0:ROWS])

                @pl.when(peer != leaf)
                def _():
                    out_copy(peer).start()

                @pl.when(peer == leaf)
                def _():
                    back[w_self] = out[peer]

            return carry

        lax.fori_loop(0, KP // BLOCK, block, 0)

    def update(k, carry):
        sum_zero, sum_one = carry
        w = lax.rem(first_worker + k, WORKERS)
        slot = lax.rem(k, 2)
        peer = worker_leaf(w)

        @pl.when(peer != leaf)
        def _():
            pltpu.make_async_remote_copy(
                src_ref=out.at[0],
                dst_ref=back.at[w],
                send_sem=out_send.at[0],
                recv_sem=out_recv.at[w],
                device_id=(line, peer),
                device_id_type=MESH,
            ).wait_recv()

        r, zs = zero_shares(rz, w, lane, hands)
        regrets, os = one_shares(ro, w, lane, hands)
        stage[slot, 0:ROWS] = decode(back[w])
        w_scale = jnp.exp2(stage[slot, 3 * hands : 3 * hands + 1]) * (1.0 / CODE)
        z_scale = jnp.exp2(stage[slot, 3 * hands + 1 : 3 * hands + 2]) * (1.0 / CODE)
        act = stage[slot, 0:hands] * w_scale
        sz = stage[slot, hands : 2 * hands] * z_scale
        dz = stage[slot, 2 * hands : 3 * hands] * z_scale
        node = action_sum(zs * act, lane)
        new_rz[pl.ds(w, hands, stride=WORKERS)] = jnp.maximum(r + act - node, 0.0)
        leaf_one = [show[b] * sz - fold[b] * dz for b in range(MOVES_ONE)]
        node_one = os[0] * leaf_one[0] + os[1] * leaf_one[1] + os[2] * leaf_one[2]
        new = [jnp.maximum(regrets[b] + leaf_one[b] - node_one, 0.0) for b in range(MOVES_ONE)]
        native = join_moves(new, lane)
        for v in range(3):
            new_ro[pl.ds(3 * w + v, hands, stride=3 * WORKERS)] = native[v]
        return (sum_zero + node, sum_one + node_one)

    zero = jnp.zeros((hands, 128), F32)
    sum_zero, sum_one = lax.fori_loop(0, WORKERS, update, (zero, zero))
    sum_zero = jnp.where(lane % 64 < SUBGAMES, sum_zero, 0.0)
    values = [
        CHANCE
        * lax.dot_general(
            tile_selector(),
            total,
            (((1,), (1,)), ((), ())),
            precision=lax.Precision.HIGHEST,
            preferred_element_type=F32,
        )
        for total in (sum_zero, sum_one)
    ]
    own[0] = turn_share * values[0]
    own[1] = values[1]
    total = line_sum(own, parts, root_send, root_recv)
    roots[...] = total
    new_turn[...] = jnp.maximum(turn_regret[...] + values[0] - total[0], 0.0)

    def y_sent(k, carry):
        w = lax.rem(first_worker + k, WORKERS)
        peer = worker_leaf(w)

        @pl.when(peer != leaf)
        def _():
            y_copy(w, peer).wait_send()

        return carry

    lax.fori_loop(0, WORKERS, y_sent, 0)

    @pl.when(is_worker)
    def _():
        def sent(k, carry):
            out_copy(lax.rem(leaf + k, PEERS)).wait_send()
            return carry

        lax.fori_loop(1, PEERS, sent, 0)

    line_sent(turn_regret, turns, turn_send, turn_recv)
    line_sent(own, parts, root_send, root_recv)


VM = pl.BlockSpec(memory_space=pltpu.VMEM)
SM = pl.BlockSpec(memory_space=pltpu.SMEM)
HB = pl.BlockSpec(memory_space=pl.ANY)
LIMIT = 56 << 20


def local(
    range_zero,
    range_one,
    turn_regret,
    river_regret_zero,
    river_regret_one,
    hand_cards,
    dealt_cards,
    hand_ranks,
    leaf_pots,
    leaf_kinds,
):
    hands = range_zero.shape[1]
    lines = lax.axis_size("river")
    tr = turn_regret[0]
    rz = river_regret_zero.reshape(hands * WORKERS, 128)
    ro = river_regret_one.reshape(hands * 3 * WORKERS, 128)
    dma = pltpu.SemaphoreType.DMA
    i16 = jnp.int16
    new_turn, new_rz, new_ro, roots = pl.pallas_call(
        kernel,
        out_shape=(
            jax.ShapeDtypeStruct(tr.shape, F32),
            jax.ShapeDtypeStruct(rz.shape, F32),
            jax.ShapeDtypeStruct(ro.shape, F32),
            jax.ShapeDtypeStruct((2,) + tr.shape, F32),
        ),
        in_specs=[HB, HB, VM, VM, VM, VM, VM, SM, SM, SM],
        out_specs=(VM, VM, VM, VM),
        scratch_shapes=[
            pltpu.VMEM(rz.shape, F32),
            pltpu.VMEM(ro.shape, F32),
            pltpu.VMEM((lines,) + tr.shape, F32),
            pltpu.VMEM((WORKERS, ROWS, 128), i16),
            pltpu.VMEM((PEERS, ROWS, 128), i16),
            pltpu.VMEM((BLOCK // HP, STAGE, 128), F32),
            pltpu.VMEM((PEERS * hands, KP), BF16),
            pltpu.VMEM((8, PEERS * hands), F32),
            pltpu.VMEM((8, KP), F32),
            pltpu.VMEM((KP, 640), BF16),
            pltpu.VMEM((3, KP, KP), BF16),
            pltpu.VMEM((3, KP, 128), F32),
            pltpu.VMEM((KP, 128), BF16),
            pltpu.VMEM((PEERS, ROWS, 128), i16),
            pltpu.VMEM((WORKERS, ROWS, 128), i16),
            pltpu.VMEM((2,) + tr.shape, F32),
            pltpu.VMEM((lines, 2) + tr.shape, F32),
            dma((2,)),
            dma((lines,)),
            dma((lines,)),
            dma((WORKERS,)),
            dma((PEERS,)),
            dma((PEERS,)),
            dma((WORKERS,)),
            dma((lines,)),
            dma((lines,)),
        ],
        compiler_params=pltpu.CompilerParams(
            collective_id=1, has_side_effects=True, vmem_limit_bytes=LIMIT
        ),
    )(
        rz,
        ro,
        range_zero,
        range_one,
        tr,
        hand_cards.T,
        hand_ranks,
        dealt_cards,
        leaf_pots,
        leaf_kinds,
    )
    return (
        new_turn[None],
        new_rz.reshape(river_regret_zero.shape),
        new_ro.reshape(river_regret_one.shape),
        roots,
    )


def solution(mesh):
    placed = (
        P(None, "leaf"),
        P(None, "leaf"),
        P("river", None, "leaf"),
        P("river", "leaf", None),
        P("river", "leaf", None),
        P(),
        P(),
        P(),
        P("river", None),
        P("river", None),
    )
    return jax.shard_map(
        local,
        mesh=mesh,
        in_specs=placed,
        out_specs=(
            P("river", None, "leaf"),
            P("river", "leaf", None),
            P("river", "leaf", None),
            P(None, None, "leaf"),
        ),
        check_vma=False,
    )
```

time: 102 us -> 89.5 us (0.88)
  local copies, waits for them, and re-layouts: 13.8 us -> 6.41 us
  Pallas kernels: 87.2 us -> 81.9 us
    pallas_call x3 -> x1, Pallas kernels: 87.2 us -> 81.9 us  [local(): pl.pallas_call(kernel, out_shape=(jax.ShapeDtypeStruct(tr.shape, F32), ja...]
    unnamed x26 -> x6, local copies, waits for them, and re-layouts: 11.4 us -> 6.41 us
    pad x2 -> x0, local copies, waits for them, and re-layouts: 1.25 us -> none  [the longest x1 0.63 us: local(): cards = jnp.pad(cards.astype(F32), ((0, 6), (0, 0)))]
where the time goes in v3:
time: 89.5 us; the launch traced here: 89 us
  Pallas kernels  81.9 us (92%)
  local copies, waits for them, and re-layouts  6.41 us (7%)
    pallas_call x1, Pallas kernels, local(): pl.pallas_call(kernel, out_shape=(jax.ShapeDtypeStruct(tr.shape, F32), ja...  81.9 us
    unnamed x6, local copies, waits for them, and re-layouts  6.41 us

profile of v3, /device:TPU:38, one launch (start us, length us, event | category | flops | bytes accessed | tf_op | source)
XLA Modules:
  0.0 89.0 jit_solution(7396336974361696186)
XLA Ops:
  0.6 81.9 %shard_map.129 = (f32[16,42]{1,0:T(8,128)}, f32[1008,128]{1,0:T(8,128)}, f32[3024,128]{1,0:T(8,128)}, f32[2,16,42]{2,1,0:T(8,128)}) custom-call(f32[1008,128]{1,0:T(8,128)} %bitcast.10, f32[3024,128]{1,0:T(8,128)} %bitcast.8, f32[16,42]{1,0:T(8,128)} %range_zero.1, f32[16,42]{1,0:T(8,128)} %range_one.1, f32[16,42]{1,0:T(8,128)} %bitcast.12, ...), custom_call_target="tpu_custom_call" | custom-call | tf_op jit(solution)/shard_map/pallas_call | solution.py:569
  82.5 1.3 %copy.22 = f32[1,16,42]{2,1,0:T(8,128)} copy(f32[1,16,42]{2,1,0:T(8,128)} %bitcast.13) | data formatting | bytes 5376
  83.8 1.9 %copy.23 = f32[1,42,3072]{2,0,1:T(1,128)} copy(f32[1,42,3072]{2,0,1:T(1,128)} %bitcast.9) | data formatting | bytes 1032192
  85.7 0.0 copy-start
  85.7 2.6 %copy.24 = f32[1,42,9216]{2,0,1:T(1,128)} copy(f32[1,42,9216]{2,0,1:T(1,128)} %bitcast.7) | data formatting | bytes 3096576
  88.3 0.0 copy-done
  88.3 0.6 copy.25
Async XLA Ops:
  85.7 2.6 %copy-start = (f32[2,16,42]{2,1,0:T(8,128)S(1)}, f32[2,16,42]{2,1,0:T(8,128)}, u32[]{:S(2)}) copy-start(f32[2,16,42]{2,1,0:T(8,128)} %get-tuple-element.27) | copy-start | bytes 16132

commit v4 on v3

--- a/solution.py
+++ b/solution.py
@@ -21,17 +21,22 @@
 CHANCE = 1.0 / 44.0
 
 
-def worker_leaf(w):
+def worker_leaf(w, line):
     z = w // 3
-    x = lax.rem(w - 3 * z + 1 + z, 4)
+    x = lax.rem(w - 3 * z + 1 + z + 2 * lax.rem(line, 2), 4)
     return 4 * z + x
 
 
-def leaf_worker(leaf):
+def leaf_worker(leaf, line):
     z = leaf // 4
     x = leaf - 4 * z
-    k = lax.rem(x - 1 - z + 12, 4)
+    k = lax.rem(x - 1 - z - 2 * lax.rem(line, 2) + 16, 4)
     return k, 3 * z + k
+
+
+def far_first(k, half):
+    h = (k + 1) // 2
+    return half + h * (1 - 2 * lax.rem(k, 2))
 
 
 def lanes(rows):
@@ -160,14 +165,17 @@
     pots,
     kinds,
     new_turn,
-    new_rz,
-    new_ro,
+    rz_out,
+    ro_out,
     roots,
     rz,
     ro,
+    new_rz,
+    new_ro,
     turns,
     yq,
     recv,
+    y_stage,
     stage,
     spread,
     card_pad,
@@ -192,10 +200,15 @@
 ):
     line, leaf = lax.axis_index("river"), lax.axis_index("leaf")
     lines = turns.shape[0]
-    k_self, w_self = leaf_worker(leaf)
+    k_self, w_self = leaf_worker(leaf, line)
     is_worker = k_self < 3
     hands = turn_regret.shape[1]
-    first_worker = 3 * (leaf // 4)
+    z_self = leaf // 4
+    x_self = leaf - 4 * z_self
+
+    def forward_worker(k):
+        step = far_first(k // 3, 4)
+        return 3 * lax.rem(z_self + step, 8) + lax.rem(k + x_self, 3)
 
     loads = [
         pltpu.make_async_copy(rz_hbm, rz, load_sem.at[0]),
@@ -226,6 +239,7 @@
     fold = [f[0:1] for f in fold]
     unit = CODE / ONE_TOP
     stage[...] = jnp.zeros_like(stage)
+    y_stage[:, 120:ROWS] = jnp.zeros((WORKERS, ROWS - 120, 128), F32)
     for load in loads:
         load.wait()
     pl.semaphore_wait(barrier, PEERS - 1 + lines - 1)
@@ -240,12 +254,14 @@
             device_id_type=MESH,
         )
 
-    def line_sum(src, dst, sends, recvs):
+    def line_start(src, dst, sends, recvs):
         def start(k, carry):
             line_copy(src, dst, sends, recvs, lax.rem(line + k, lines), line).start()
             return carry
 
         lax.fori_loop(1, lines, start, 0)
+
+    def line_sum(src, dst, sends, recvs):
         dst[line] = src[...]
 
         def wait(k, carry):
@@ -266,6 +282,17 @@
 
         lax.fori_loop(1, lines, wait, 0)
 
+    line_start(turn_regret, turns, turn_send, turn_recv)
+
+    def prepare_one(w, carry):
+        _, os = one_shares(ro, w, lane, hands)
+        o = [(weight_one * s).astype(BF16).astype(F32) for s in os]
+        for j, scale in enumerate((show, fold)):
+            mixed = o[0] * scale[0] + o[1] * scale[1] + o[2] * scale[2]
+            y_stage[w, (j + 1) * hands : (j + 2) * hands] = nearest(mixed * unit)
+        return carry
+
+    lax.fori_loop(0, WORKERS, prepare_one, 0)
     turn_share = turn_regret[...] / line_sum(turn_regret, turns, turn_send, turn_recv)
     weight_zero = to_lanes(range_zero[...] * turn_share)
 
@@ -280,20 +307,14 @@
         )
 
     def prepare(k, carry):
-        w = lax.rem(first_worker + k, WORKERS)
-        slot = lax.rem(k, 2)
+        w = forward_worker(k)
         _, zs = zero_shares(rz, w, lane, hands)
-        _, os = one_shares(ro, w, lane, hands)
         z = (weight_zero * zs).astype(BF16).astype(F32)
         power = power_above(jnp.max(z, axis=0, keepdims=True))
-        o = [(weight_one * s).astype(BF16).astype(F32) for s in os]
-        stage[slot, 0:hands] = nearest(z * (CODE * jnp.exp2(-power)))
-        for j, scale in enumerate((show, fold)):
-            mixed = o[0] * scale[0] + o[1] * scale[1] + o[2] * scale[2]
-            stage[slot, (j + 1) * hands : (j + 2) * hands] = nearest(mixed * unit)
-        stage[slot, 3 * hands : 3 * hands + 1] = power
-        yq[w] = code(stage[slot, 0:ROWS])
-        peer = worker_leaf(w)
+        y_stage[w, 0:hands] = nearest(z * (CODE * jnp.exp2(-power)))
+        y_stage[w, 3 * hands : 3 * hands + 1] = power
+        yq[w] = code(y_stage[w, 0:ROWS])
+        peer = worker_leaf(w, line)
 
         @pl.when(peer != leaf)
         def _():
@@ -381,10 +402,11 @@
 
         def arrive(k, carry):
             z_sum, w_sum = carry
-            source = lax.rem(leaf + k, PEERS)
+            source_z = lax.rem(z_self - far_first(k // 4, 4) + 16, 8)
+            source = 4 * source_z + lax.rem(k + x_self, 4)
             slot = lax.rem(k, 2)
 
-            @pl.when(k > 0)
+            @pl.when(source != leaf)
             def _():
                 pltpu.make_async_remote_copy(
                     src_ref=yq.at[0],
@@ -423,7 +445,7 @@
         low_part = jnp.where(low, 256.0, 1.0)
 
         def block(k, carry):
-            i = lax.rem(leaf // (BLOCK // HP) + k, KP // BLOCK)
+            i = lax.rem(z_self // 2 + far_first(k, 2), 4)
             rows = pl.ds(pl.multiple_of(i * BLOCK, BLOCK), BLOCK)
             d = jnp.dot(mat[2, rows], x[:, 0:384], preferred_element_type=F32)
             s0z = jnp.dot(mat[0, rows], x[:, 0:128], preferred_element_type=F32)
@@ -464,9 +486,10 @@
 
     def update(k, carry):
         sum_zero, sum_one = carry
-        w = lax.rem(first_worker + k, WORKERS)
+        pair = lax.rem(z_self // 2 - far_first(k // 6, 2) + 8, 4)
+        w = 6 * pair + lax.rem(k, 6)
         slot = lax.rem(k, 2)
-        peer = worker_leaf(w)
+        peer = worker_leaf(w, line)
 
         @pl.when(peer != leaf)
         def _():
@@ -499,6 +522,12 @@
 
     zero = jnp.zeros((hands, 128), F32)
     sum_zero, sum_one = lax.fori_loop(0, WORKERS, update, (zero, zero))
+    stores = [
+        pltpu.make_async_copy(new_rz, rz_out, load_sem.at[2]),
+        pltpu.make_async_copy(new_ro, ro_out, load_sem.at[3]),
+    ]
+    for store in stores:
+        store.start()
     sum_zero = jnp.where(lane % 64 < SUBGAMES, sum_zero, 0.0)
     values = [
         CHANCE
@@ -513,13 +542,14 @@
     ]
     own[0] = turn_share * values[0]
     own[1] = values[1]
+    line_start(own, parts, root_send, root_recv)
     total = line_sum(own, parts, root_send, root_recv)
     roots[...] = total
     new_turn[...] = jnp.maximum(turn_regret[...] + values[0] - total[0], 0.0)
 
     def y_sent(k, carry):
-        w = lax.rem(first_worker + k, WORKERS)
-        peer = worker_leaf(w)
+        w = forward_worker(k)
+        peer = worker_leaf(w, line)
 
         @pl.when(peer != leaf)
         def _():
@@ -539,6 +569,24 @@
 
     line_sent(turn_regret, turns, turn_send, turn_recv)
     line_sent(own, parts, root_send, root_recv)
+    for store in stores:
+        store.wait()
+
+
+def place_kernel(*refs):
+    count = (len(refs) - 2) // 3
+    srcs, dsts, held = refs[:count], refs[count : 2 * count], refs[2 * count : 3 * count]
+    load_sem, store_sem = refs[-2], refs[-1]
+    loads, stores = [], []
+    for k in range(count):
+        loads.append(pltpu.make_async_copy(srcs[k], held[k], load_sem.at[k]))
+        stores.append(pltpu.make_async_copy(held[k], dsts[k], store_sem.at[k]))
+        loads[k].start()
+    for k in range(count):
+        loads[k].wait()
+        stores[k].start()
+    for k in range(count):
+        stores[k].wait()
 
 
 VM = pl.BlockSpec(memory_space=pltpu.VMEM)
@@ -575,13 +623,16 @@
             jax.ShapeDtypeStruct((2,) + tr.shape, F32),
         ),
         in_specs=[HB, HB, VM, VM, VM, VM, VM, SM, SM, SM],
-        out_specs=(VM, VM, VM, VM),
+        out_specs=(VM, HB, HB, VM),
         scratch_shapes=[
+            pltpu.VMEM(rz.shape, F32),
+            pltpu.VMEM(ro.shape, F32),
             pltpu.VMEM(rz.shape, F32),
             pltpu.VMEM(ro.shape, F32),
             pltpu.VMEM((lines,) + tr.shape, F32),
             pltpu.VMEM((WORKERS, ROWS, 128), i16),
             pltpu.VMEM((PEERS, ROWS, 128), i16),
+            pltpu.VMEM((WORKERS, ROWS, 128), F32),
             pltpu.VMEM((BLOCK // HP, STAGE, 128), F32),
             pltpu.VMEM((PEERS * hands, KP), BF16),
             pltpu.VMEM((8, PEERS * hands), F32),
@@ -594,7 +645,7 @@
             pltpu.VMEM((WORKERS, ROWS, 128), i16),
             pltpu.VMEM((2,) + tr.shape, F32),
             pltpu.VMEM((lines, 2) + tr.shape, F32),
-            dma((2,)),
+            dma((4,)),
             dma((lines,)),
             dma((lines,)),
             dma((WORKERS,)),
@@ -619,6 +670,14 @@
         leaf_pots,
         leaf_kinds,
     )
+    results = (new_turn, new_rz, new_ro, roots)
+    new_turn, new_rz, new_ro, roots = pl.pallas_call(
+        place_kernel,
+        out_shape=tuple(jax.ShapeDtypeStruct(r.shape, F32) for r in results),
+        in_specs=[HB] * 4,
+        out_specs=(HB,) * 4,
+        scratch_shapes=[pltpu.VMEM(r.shape, F32) for r in results] + [dma((4,)), dma((4,))],
+    )(*results)
     return (
         new_turn[None],
         new_rz.reshape(river_regret_zero.shape),

time: 89.5 us -> 75.8 us (0.85)
  Pallas kernels: 81.9 us -> 74.9 us
  local copies, waits for them, and re-layouts: 6.41 us -> 0 us
    pallas_call x1, Pallas kernels: 81.9 us -> 72.1 us  [local(): pl.pallas_call(kernel, out_shape=(jax.ShapeDtypeStruct(tr.shape, F32), ja...]
    unnamed x6 -> x0, local copies, waits for them, and re-layouts: 6.41 us -> none
    pallas_call x0 -> x1, Pallas kernels: none -> 2.79 us  [local(): pl.pallas_call(place_kernel, out_shape=tuple((jax.ShapeDtypeStruct(r.shap...]
where the time goes in v4:
time: 75.8 us; the launch traced here: 75.6 us
  Pallas kernels  74.9 us (99%)
    pallas_call x1, Pallas kernels, local(): pl.pallas_call(kernel, out_shape=(jax.ShapeDtypeStruct(tr.shape, F32), ja...  72.1 us
    pallas_call x1, Pallas kernels, local(): pl.pallas_call(place_kernel, out_shape=tuple((jax.ShapeDtypeStruct(r.shap...  2.79 us

profile of v4, /device:TPU:38, one launch (start us, length us, event | category | flops | bytes accessed | tf_op | source)
XLA Modules:
  0.0 75.6 jit_solution(16057692423402163084)
XLA Ops:
  0.6 72.1 %shard_map.129 = (f32[16,42]{1,0:T(8,128)}, f32[1008,128]{1,0:T(8,128)}, f32[3024,128]{1,0:T(8,128)}, f32[2,16,42]{2,1,0:T(8,128)}) custom-call(f32[1008,128]{1,0:T(8,128)} %bitcast.8, f32[3024,128]{1,0:T(8,128)} %bitcast.7, f32[16,42]{1,0:T(8,128)} %range_zero.1, f32[16,42]{1,0:T(8,128)} %range_one.1, f32[16,42]{1,0:T(8,128)} %bitcast.10, ...), custom_call_target="tpu_custom_call" | custom-call | tf_op jit(solution)/shard_map/pallas_call | solution.py:617
  72.8 2.8 %shard_map.130 = (f32[16,42]{1,0:T(8,128)}, f32[1008,128]{1,0:T(8,128)}, f32[3024,128]{1,0:T(8,128)}, f32[2,16,42]{2,1,0:T(8,128)}) custom-call(f32[16,42]{1,0:T(8,128)} %get-tuple-element.12.refs_0_, f32[1008,128]{1,0:T(8,128)} %get-tuple-element.13.refs_1_, f32[3024,128]{1,0:T(8,128)} %get-tuple-element.14.refs_2_, f32[2,16,42]{2,1,0:T(8,128)} %get-tuple-element.15.refs_3_), custom_call_target="tpu_custom_call" | custom-call | tf_op jit(solution)/shard_map/pallas_call | solution.py:674

commit v5 on v4

--- a/solution.py
+++ b/solution.py
@@ -117,6 +117,8 @@
 CODE = 32760.0
 ROWS = 128
 STAGE = 136
+SPLIT = 80
+EARLY = 16
 
 
 def column(rows, select):
@@ -146,11 +148,10 @@
     return x, x / action_sum(x, lane)
 
 
-def one_shares(ro, w, lane, hands):
+def one_regrets(ro, w, lane, hands):
     tiles = [ro[pl.ds(3 * w + v, hands, stride=3 * WORKERS)] for v in range(3)]
     regrets = split_moves(tiles, lane)
-    scale = 1.0 / (regrets[0] + regrets[1] + regrets[2])
-    return regrets, [r * scale for r in regrets]
+    return regrets, 1.0 / (regrets[0] + regrets[1] + regrets[2])
 
 
 def kernel(
@@ -175,6 +176,7 @@
     turns,
     yq,
     recv,
+    kept,
     y_stage,
     stage,
     spread,
@@ -284,49 +286,59 @@
 
     line_start(turn_regret, turns, turn_send, turn_recv)
 
-    def prepare_one(w, carry):
-        _, os = one_shares(ro, w, lane, hands)
-        o = [(weight_one * s).astype(BF16).astype(F32) for s in os]
-        for j, scale in enumerate((show, fold)):
-            mixed = o[0] * scale[0] + o[1] * scale[1] + o[2] * scale[2]
-            y_stage[w, (j + 1) * hands : (j + 2) * hands] = nearest(mixed * unit)
+    def y_copy(part, w, peer, slot):
+        rows = (pl.ds(0, SPLIT), pl.ds(SPLIT, ROWS - SPLIT))[part]
+        return pltpu.make_async_remote_copy(
+            src_ref=yq.at[w, rows],
+            dst_ref=recv.at[slot, rows],
+            send_sem=y_send.at[part, w],
+            recv_sem=y_recv.at[part, slot],
+            device_id=(line, peer),
+            device_id_type=MESH,
+        )
+
+    def hand_over(part, w):
+        peer = worker_leaf(w, line)
+        rows = (pl.ds(0, SPLIT), pl.ds(SPLIT, ROWS - SPLIT))[part]
+        yq[w, rows] = code(y_stage[w, rows])
+
+        @pl.when(peer != leaf)
+        def _():
+            y_copy(part, w, peer, leaf).start()
+
+        @pl.when(peer == leaf)
+        def _():
+            recv[leaf, rows] = yq[w, rows]
+
+    def prepare_one(k, carry):
+        w = forward_worker(k)
+        regrets, scale = one_regrets(ro, w, lane, hands)
+        for b in range(MOVES_ONE):
+            kept[w, b, 0:hands] = regrets[b]
+        kept[w, 3, 0:hands] = scale
+        o = [(weight_one * (r * scale)).astype(BF16).astype(F32) for r in regrets]
+        for j, pot in enumerate((show, fold)):
+            mixed = o[0] * pot[0] + o[1] * pot[1] + o[2] * pot[2]
+            y_stage[w, j * hands : (j + 1) * hands] = nearest(mixed * unit)
+        hand_over(0, w)
         return carry
 
     lax.fori_loop(0, WORKERS, prepare_one, 0)
     turn_share = turn_regret[...] / line_sum(turn_regret, turns, turn_send, turn_recv)
     weight_zero = to_lanes(range_zero[...] * turn_share)
 
-    def y_copy(w, peer):
-        return pltpu.make_async_remote_copy(
-            src_ref=yq.at[w],
-            dst_ref=recv.at[leaf],
-            send_sem=y_send.at[w],
-            recv_sem=y_recv.at[leaf],
-            device_id=(line, peer),
-            device_id_type=MESH,
-        )
-
-    def prepare(k, carry):
+    def prepare_zero(k, carry):
         w = forward_worker(k)
         _, zs = zero_shares(rz, w, lane, hands)
+        kept[w, 4, 0:hands] = zs
         z = (weight_zero * zs).astype(BF16).astype(F32)
         power = power_above(jnp.max(z, axis=0, keepdims=True))
-        y_stage[w, 0:hands] = nearest(z * (CODE * jnp.exp2(-power)))
+        y_stage[w, 2 * hands : 3 * hands] = nearest(z * (CODE * jnp.exp2(-power)))
         y_stage[w, 3 * hands : 3 * hands + 1] = power
-        yq[w] = code(y_stage[w, 0:ROWS])
-        peer = worker_leaf(w, line)
-
-        @pl.when(peer != leaf)
-        def _():
-            y_copy(w, peer).start()
-
-        @pl.when(peer == leaf)
-        def _():
-            recv[leaf] = yq[w]
-
+        hand_over(1, w)
         return carry
 
-    lax.fori_loop(0, WORKERS, prepare, 0)
+    lax.fori_loop(0, WORKERS, prepare_zero, 0)
 
     def out_copy(peer):
         return pltpu.make_async_remote_copy(
@@ -400,44 +412,44 @@
 
         lax.fori_loop(0, KP // MB, build, 0)
 
-        def arrive(k, carry):
-            z_sum, w_sum = carry
+        def arrival(part, k):
             source_z = lax.rem(z_self - far_first(k // 4, 4) + 16, 8)
             source = 4 * source_z + lax.rem(k + x_self, 4)
-            slot = lax.rem(k, 2)
 
             @pl.when(source != leaf)
             def _():
-                pltpu.make_async_remote_copy(
-                    src_ref=yq.at[0],
-                    dst_ref=recv.at[source],
-                    send_sem=y_send.at[0],
-                    recv_sem=y_recv.at[source],
-                    device_id=(line, source),
-                    device_id_type=MESH,
-                ).wait_recv()
+                y_copy(part, 0, source, source).wait_recv()
 
             rows = pl.ds(pl.multiple_of(source * HP, HP), HP)
-            v = col[2, rows]
-            coded = decode(recv[source])
-            stage[slot, 0:ROWS] = coded
-            scale = jnp.exp2(stage[slot, 3 * hands : 3 * hands + 1]) * (1.0 / CODE)
-            z = (stage[slot, 0:HP] * (v * scale)).astype(BF16)
-            ws = stage[slot, hands : hands + HP] * v
-            wf = stage[slot, 2 * hands : 2 * hands + HP] * v
+            return source, rows, col[2, rows]
+
+        def arrive_one(k, w_sum):
+            source, rows, v = arrival(0, k)
+            ws = decode(recv[source, 0:HP]) * v
             s_high = jnp.floor(ws * (1.0 / 256.0))
             s_low = ws - 256.0 * s_high
+            x[rows, 384:512] = jnp.where(low, s_high, roll_half(s_low)).astype(BF16)
+            x[rows, 512:640] = jnp.where(low, roll_half(s_high), s_low).astype(BF16)
+            return w_sum + ws
+
+        def arrive_two(k, carry):
+            z_sum, w_sum = carry
+            source, rows, v = arrival(1, k)
+            slot = lax.rem(k, 2)
+            stage[slot, 32:ROWS] = decode(recv[source, 32:ROWS])
+            scale = jnp.exp2(stage[slot, 3 * hands : 3 * hands + 1]) * (1.0 / CODE)
+            wf = stage[slot, hands : hands + HP] * v
+            z = (stage[slot, 2 * hands : 2 * hands + HP] * (v * scale)).astype(BF16)
             f_high = jnp.floor(wf * (1.0 / 256.0))
             f_low = wf - 256.0 * f_high
             x[rows, 0:128] = z
             x[rows, 128:256] = f_high.astype(BF16)
             x[rows, 256:384] = f_low.astype(BF16)
-            x[rows, 384:512] = jnp.where(low, s_high, roll_half(s_low)).astype(BF16)
-            x[rows, 512:640] = jnp.where(low, roll_half(s_high), s_low).astype(BF16)
-            return (z_sum + z.astype(F32), w_sum + ws + jnp.abs(wf))
+            return (z_sum + z.astype(F32), w_sum + jnp.abs(wf))
 
         empty = jnp.zeros((HP, 128), F32)
-        z_sum, w_sum = lax.fori_loop(0, PEERS, arrive, (empty, empty))
+        w_sum = lax.fori_loop(0, PEERS, arrive_one, empty)
+        z_sum, w_sum = lax.fori_loop(0, PEERS, arrive_two, (empty, w_sum))
         z_power = power_above(jnp.sum(z_sum, axis=0, keepdims=True))
         w_power = power_above(jnp.sum(w_sum, axis=0, keepdims=True) * (1.0 / unit))
         z_scale = CODE * jnp.exp2(-z_power)
@@ -484,11 +496,25 @@
 
         lax.fori_loop(0, KP // BLOCK, block, 0)
 
-    def update(k, carry):
-        sum_zero, sum_one = carry
+    def values_of(k):
         pair = lax.rem(z_self // 2 - far_first(k // 6, 2) + 8, 4)
         w = 6 * pair + lax.rem(k, 6)
         slot = lax.rem(k, 2)
+        stage[slot, 0:ROWS] = decode(back[w])
+        w_scale = jnp.exp2(stage[slot, 3 * hands : 3 * hands + 1]) * (1.0 / CODE)
+        z_scale = jnp.exp2(stage[slot, 3 * hands + 1 : 3 * hands + 2]) * (1.0 / CODE)
+        act = stage[slot, 0:hands] * w_scale
+        sz = stage[slot, hands : 2 * hands] * z_scale
+        dz = stage[slot, 2 * hands : 3 * hands] * z_scale
+        node = action_sum(kept[w, 4, 0:hands] * act, lane)
+        regrets = [kept[w, b, 0:hands] for b in range(MOVES_ONE)]
+        leaf_one = [show[b] * sz - fold[b] * dz for b in range(MOVES_ONE)]
+        node_one = regrets[0] * leaf_one[0] + regrets[1] * leaf_one[1] + regrets[2] * leaf_one[2]
+        return w, act, node, regrets, leaf_one, node_one * kept[w, 3, 0:hands]
+
+    def collect(k, carry):
+        pair = lax.rem(z_self // 2 - far_first(k // 6, 2) + 8, 4)
+        w = 6 * pair + lax.rem(k, 6)
         peer = worker_leaf(w, line)
 
         @pl.when(peer != leaf)
@@ -502,32 +528,35 @@
                 device_id_type=MESH,
             ).wait_recv()
 
-        r, zs = zero_shares(rz, w, lane, hands)
-        regrets, os = one_shares(ro, w, lane, hands)
-        stage[slot, 0:ROWS] = decode(back[w])
-        w_scale = jnp.exp2(stage[slot, 3 * hands : 3 * hands + 1]) * (1.0 / CODE)
-        z_scale = jnp.exp2(stage[slot, 3 * hands + 1 : 3 * hands + 2]) * (1.0 / CODE)
-        act = stage[slot, 0:hands] * w_scale
-        sz = stage[slot, hands : 2 * hands] * z_scale
-        dz = stage[slot, 2 * hands : 3 * hands] * z_scale
-        node = action_sum(zs * act, lane)
+        return carry
+
+    def renew(values):
+        w, act, node, regrets, leaf_one, node_one = values
+        r = rz[pl.ds(w, hands, stride=WORKERS)]
         new_rz[pl.ds(w, hands, stride=WORKERS)] = jnp.maximum(r + act - node, 0.0)
-        leaf_one = [show[b] * sz - fold[b] * dz for b in range(MOVES_ONE)]
-        node_one = os[0] * leaf_one[0] + os[1] * leaf_one[1] + os[2] * leaf_one[2]
         new = [jnp.maximum(regrets[b] + leaf_one[b] - node_one, 0.0) for b in range(MOVES_ONE)]
         native = join_moves(new, lane)
         for v in range(3):
             new_ro[pl.ds(3 * w + v, hands, stride=3 * WORKERS)] = native[v]
-        return (sum_zero + node, sum_one + node_one)
+
+    def update(k, carry):
+        collect(k, 0)
+        values = values_of(k)
+        renew(values)
+        return (carry[0] + values[2], carry[1] + values[5])
+
+    def sum_only(k, carry):
+        collect(k, 0)
+        values = values_of(k)
+        return (carry[0] + values[2], carry[1] + values[5])
+
+    def finish(k, carry):
+        renew(values_of(k))
+        return carry
 
     zero = jnp.zeros((hands, 128), F32)
-    sum_zero, sum_one = lax.fori_loop(0, WORKERS, update, (zero, zero))
-    stores = [
-        pltpu.make_async_copy(new_rz, rz_out, load_sem.at[2]),
-        pltpu.make_async_copy(new_ro, ro_out, load_sem.at[3]),
-    ]
-    for store in stores:
-        store.start()
+    sums = lax.fori_loop(0, EARLY, update, (zero, zero))
+    sum_zero, sum_one = lax.fori_loop(EARLY, WORKERS, sum_only, sums)
     sum_zero = jnp.where(lane % 64 < SUBGAMES, sum_zero, 0.0)
     values = [
         CHANCE
@@ -543,6 +572,13 @@
     own[0] = turn_share * values[0]
     own[1] = values[1]
     line_start(own, parts, root_send, root_recv)
+    lax.fori_loop(EARLY, WORKERS, finish, 0)
+    stores = [
+        pltpu.make_async_copy(new_rz, rz_out, load_sem.at[2]),
+        pltpu.make_async_copy(new_ro, ro_out, load_sem.at[3]),
+    ]
+    for store in stores:
+        store.start()
     total = line_sum(own, parts, root_send, root_recv)
     roots[...] = total
     new_turn[...] = jnp.maximum(turn_regret[...] + values[0] - total[0], 0.0)
@@ -553,7 +589,8 @@
 
         @pl.when(peer != leaf)
         def _():
-            y_copy(w, peer).wait_send()
+            y_copy(0, w, peer, leaf).wait_send()
+            y_copy(1, w, peer, leaf).wait_send()
 
         return carry
 
@@ -632,6 +669,7 @@
             pltpu.VMEM((lines,) + tr.shape, F32),
             pltpu.VMEM((WORKERS, ROWS, 128), i16),
             pltpu.VMEM((PEERS, ROWS, 128), i16),
+            pltpu.VMEM((WORKERS, 5, HP, 128), F32),
             pltpu.VMEM((WORKERS, ROWS, 128), F32),
             pltpu.VMEM((BLOCK // HP, STAGE, 128), F32),
             pltpu.VMEM((PEERS * hands, KP), BF16),
@@ -648,8 +686,8 @@
             dma((4,)),
             dma((lines,)),
             dma((lines,)),
-            dma((WORKERS,)),
-            dma((PEERS,)),
+            dma((2, WORKERS)),
+            dma((2, PEERS)),
             dma((PEERS,)),
             dma((WORKERS,)),
             dma((lines,)),

time: 75.8 us -> 70.4 us (0.929)
  Pallas kernels: 74.9 us -> 69.3 us
    pallas_call x1, Pallas kernels: 72.1 us -> 66.5 us  [local(): pl.pallas_call(kernel, out_shape=(jax.ShapeDtypeStruct(tr.shape, F32), ja...]
where the time goes in v5:
time: 70.4 us; the launch traced here: 70 us
  Pallas kernels  69.3 us (98%)
    pallas_call x1, Pallas kernels, local(): pl.pallas_call(kernel, out_shape=(jax.ShapeDtypeStruct(tr.shape, F32), ja...  66.5 us
    pallas_call x1, Pallas kernels, local(): pl.pallas_call(place_kernel, out_shape=tuple((jax.ShapeDtypeStruct(r.shap...  2.79 us

profile of v5, /device:TPU:38, one launch (start us, length us, event | category | flops | bytes accessed | tf_op | source)
XLA Modules:
  0.0 70.0 jit_solution(16538264526827706488)
XLA Ops:
  0.6 66.5 %shard_map.129 = (f32[16,42]{1,0:T(8,128)}, f32[1008,128]{1,0:T(8,128)}, f32[3024,128]{1,0:T(8,128)}, f32[2,16,42]{2,1,0:T(8,128)}) custom-call(f32[1008,128]{1,0:T(8,128)} %bitcast.8, f32[3024,128]{1,0:T(8,128)} %bitcast.7, f32[16,42]{1,0:T(8,128)} %range_zero.1, f32[16,42]{1,0:T(8,128)} %range_one.1, f32[16,42]{1,0:T(8,128)} %bitcast.10, ...), custom_call_target="tpu_custom_call" | custom-call | tf_op jit(solution)/shard_map/pallas_call | solution.py:654
  67.2 2.8 %shard_map.130 = (f32[16,42]{1,0:T(8,128)}, f32[1008,128]{1,0:T(8,128)}, f32[3024,128]{1,0:T(8,128)}, f32[2,16,42]{2,1,0:T(8,128)}) custom-call(f32[16,42]{1,0:T(8,128)} %get-tuple-element.12.refs_0_, f32[1008,128]{1,0:T(8,128)} %get-tuple-element.13.refs_1_, f32[3024,128]{1,0:T(8,128)} %get-tuple-element.14.refs_2_, f32[2,16,42]{2,1,0:T(8,128)} %get-tuple-element.15.refs_3_), custom_call_target="tpu_custom_call" | custom-call | tf_op jit(solution)/shard_map/pallas_call | solution.py:712

commit v6 on v5

--- a/solution.py
+++ b/solution.py
@@ -118,7 +118,9 @@
 ROWS = 128
 STAGE = 136
 SPLIT = 80
-EARLY = 16
+EARLY = 5
+PLANE = 4
+TRIO = 3
 
 
 def column(rows, select):
@@ -155,22 +157,30 @@
 
 
 def kernel(
+    turn_hbm,
+    ro_hbm,
+    range_one_hbm,
+    pots_hbm,
+    kinds_hbm,
     rz_hbm,
-    ro_hbm,
-    range_zero,
-    range_one,
-    turn_regret,
-    cards,
-    all_ranks,
-    dealt,
-    pots,
-    kinds,
+    range_zero_hbm,
+    cards_hbm,
+    ranks_hbm,
+    dealt_hbm,
     new_turn,
     rz_out,
     ro_out,
     roots,
+    turn_regret,
+    ro,
+    range_one,
+    pots,
+    kinds,
     rz,
-    ro,
+    range_zero,
+    cards,
+    all_ranks,
+    dealt,
     new_rz,
     new_ro,
     turns,
@@ -191,6 +201,7 @@
     own,
     parts,
     load_sem,
+    store_sem,
     turn_send,
     turn_recv,
     y_send,
@@ -212,27 +223,37 @@
         step = far_first(k // 3, 4)
         return 3 * lax.rem(z_self + step, 8) + lax.rem(k + x_self, 3)
 
+    sources = (
+        turn_hbm,
+        ro_hbm,
+        range_one_hbm,
+        pots_hbm,
+        kinds_hbm,
+        rz_hbm,
+        range_zero_hbm,
+        cards_hbm,
+        ranks_hbm,
+        dealt_hbm,
+    )
+    places = (turn_regret, ro, range_one, pots, kinds, rz, range_zero, cards, all_ranks, dealt)
     loads = [
-        pltpu.make_async_copy(rz_hbm, rz, load_sem.at[0]),
-        pltpu.make_async_copy(ro_hbm, ro, load_sem.at[1]),
+        pltpu.make_async_copy(a, b, load_sem.at[k]) for k, (a, b) in enumerate(zip(sources, places))
     ]
-    for load in loads:
+
+    barrier = pltpu.get_barrier_semaphore()
+
+    for load in loads[:2]:
         load.start()
-
-    barrier = pltpu.get_barrier_semaphore()
-
-    def greet_leaf(k, carry):
+    for k in range(1, lines):
+        peer = lax.rem(line + k, lines)
+        pl.semaphore_signal(barrier, inc=1, device_id=(peer, leaf), device_id_type=MESH)
+    for k in range(1, PEERS):
         peer = lax.rem(leaf + k, PEERS)
         pl.semaphore_signal(barrier, inc=1, device_id=(line, peer), device_id_type=MESH)
-        return carry
-
-    def greet_line(k, carry):
-        peer = lax.rem(line + k, lines)
-        pl.semaphore_signal(barrier, inc=1, device_id=(peer, leaf), device_id_type=MESH)
-        return carry
-
-    lax.fori_loop(1, lines, greet_line, 0)
-    lax.fori_loop(1, PEERS, greet_leaf, 0)
+    for load in loads[2:]:
+        load.start()
+    for load in loads:
+        load.wait()
 
     lane = lanes(hands)
     weight_one = to_lanes(range_one[...])
@@ -242,8 +263,6 @@
     unit = CODE / ONE_TOP
     stage[...] = jnp.zeros_like(stage)
     y_stage[:, 120:ROWS] = jnp.zeros((WORKERS, ROWS - 120, 128), F32)
-    for load in loads:
-        load.wait()
     pl.semaphore_wait(barrier, PEERS - 1 + lines - 1)
 
     def line_copy(src, dst, sends, recvs, peer, slot):
@@ -311,19 +330,21 @@
             recv[leaf, rows] = yq[w, rows]
 
     def prepare_one(k, carry):
-        w = forward_worker(k)
-        regrets, scale = one_regrets(ro, w, lane, hands)
-        for b in range(MOVES_ONE):
-            kept[w, b, 0:hands] = regrets[b]
-        kept[w, 3, 0:hands] = scale
-        o = [(weight_one * (r * scale)).astype(BF16).astype(F32) for r in regrets]
-        for j, pot in enumerate((show, fold)):
-            mixed = o[0] * pot[0] + o[1] * pot[1] + o[2] * pot[2]
-            y_stage[w, j * hands : (j + 1) * hands] = nearest(mixed * unit)
-        hand_over(0, w)
+        workers = [forward_worker(TRIO * k + m) for m in range(TRIO)]
+        for w in workers:
+            regrets, scale = one_regrets(ro, w, lane, hands)
+            for b in range(MOVES_ONE):
+                kept[w, b, 0:hands] = regrets[b]
+            kept[w, 3, 0:hands] = scale
+            o = [(weight_one * (r * scale)).astype(BF16).astype(F32) for r in regrets]
+            for j, pot in enumerate((show, fold)):
+                mixed = o[0] * pot[0] + o[1] * pot[1] + o[2] * pot[2]
+                y_stage[w, j * hands : (j + 1) * hands] = nearest(mixed * unit)
+        for w in workers:
+            hand_over(0, w)
         return carry
 
-    lax.fori_loop(0, WORKERS, prepare_one, 0)
+    lax.fori_loop(0, WORKERS // TRIO, prepare_one, 0)
     turn_share = turn_regret[...] / line_sum(turn_regret, turns, turn_send, turn_recv)
     weight_zero = to_lanes(range_zero[...] * turn_share)
 
@@ -413,19 +434,23 @@
         lax.fori_loop(0, KP // MB, build, 0)
 
         def arrival(part, k):
-            source_z = lax.rem(z_self - far_first(k // 4, 4) + 16, 8)
-            source = 4 * source_z + lax.rem(k + x_self, 4)
-
-            @pl.when(source != leaf)
-            def _():
-                y_copy(part, 0, source, source).wait_recv()
-
-            rows = pl.ds(pl.multiple_of(source * HP, HP), HP)
-            return source, rows, col[2, rows]
+            source_z = lax.rem(z_self - far_first(k, 4) + 16, 8)
+            for m in range(PLANE):
+                source = PLANE * source_z + m
+
+                @pl.when(source != leaf)
+                def _():
+                    y_copy(part, 0, source, source).wait_recv()
+
+            rows = pl.ds(pl.multiple_of(source_z * (PLANE * HP), PLANE * HP), PLANE * HP)
+            return pl.ds(PLANE * source_z, PLANE), rows, col[2, rows]
+
+        def flat(v):
+            return v.reshape(PLANE * HP, 128)
 
         def arrive_one(k, w_sum):
-            source, rows, v = arrival(0, k)
-            ws = decode(recv[source, 0:HP]) * v
+            sources, rows, v = arrival(0, k)
+            ws = flat(decode(recv[sources, 0:HP])) * v
             s_high = jnp.floor(ws * (1.0 / 256.0))
             s_low = ws - 256.0 * s_high
             x[rows, 384:512] = jnp.where(low, s_high, roll_half(s_low)).astype(BF16)
@@ -434,12 +459,11 @@
 
         def arrive_two(k, carry):
             z_sum, w_sum = carry
-            source, rows, v = arrival(1, k)
-            slot = lax.rem(k, 2)
-            stage[slot, 32:ROWS] = decode(recv[source, 32:ROWS])
-            scale = jnp.exp2(stage[slot, 3 * hands : 3 * hands + 1]) * (1.0 / CODE)
-            wf = stage[slot, hands : hands + HP] * v
-            z = (stage[slot, 2 * hands : 2 * hands + HP] * (v * scale)).astype(BF16)
+            sources, rows, v = arrival(1, k)
+            stage[0:PLANE, 32:ROWS] = decode(recv[sources, 32:ROWS])
+            scale = jnp.exp2(stage[0:PLANE, 3 * hands : 3 * hands + 1]) * (1.0 / CODE)
+            wf = flat(stage[0:PLANE, hands : hands + HP]) * v
+            z = (flat(stage[0:PLANE, 2 * hands : 2 * hands + HP] * scale) * v).astype(BF16)
             f_high = jnp.floor(wf * (1.0 / 256.0))
             f_low = wf - 256.0 * f_high
             x[rows, 0:128] = z
@@ -447,9 +471,9 @@
             x[rows, 256:384] = f_low.astype(BF16)
             return (z_sum + z.astype(F32), w_sum + jnp.abs(wf))
 
-        empty = jnp.zeros((HP, 128), F32)
-        w_sum = lax.fori_loop(0, PEERS, arrive_one, empty)
-        z_sum, w_sum = lax.fori_loop(0, PEERS, arrive_two, (empty, w_sum))
+        empty = jnp.zeros((PLANE * HP, 128), F32)
+        w_sum = lax.fori_loop(0, PEERS // PLANE, arrive_one, empty)
+        z_sum, w_sum = lax.fori_loop(0, PEERS // PLANE, arrive_two, (empty, w_sum))
         z_power = power_above(jnp.sum(z_sum, axis=0, keepdims=True))
         w_power = power_above(jnp.sum(w_sum, axis=0, keepdims=True) * (1.0 / unit))
         z_scale = CODE * jnp.exp2(-z_power)
@@ -496,10 +520,11 @@
 
         lax.fori_loop(0, KP // BLOCK, block, 0)
 
-    def values_of(k):
-        pair = lax.rem(z_self // 2 - far_first(k // 6, 2) + 8, 4)
-        w = 6 * pair + lax.rem(k, 6)
-        slot = lax.rem(k, 2)
+    def first_of(k):
+        pair = lax.rem(z_self // 2 - far_first(k // 2, 2) + 8, 4)
+        return TRIO * (2 * pair + lax.rem(k, 2))
+
+    def values_of(w, slot):
         stage[slot, 0:ROWS] = decode(back[w])
         w_scale = jnp.exp2(stage[slot, 3 * hands : 3 * hands + 1]) * (1.0 / CODE)
         z_scale = jnp.exp2(stage[slot, 3 * hands + 1 : 3 * hands + 2]) * (1.0 / CODE)
@@ -512,9 +537,7 @@
         node_one = regrets[0] * leaf_one[0] + regrets[1] * leaf_one[1] + regrets[2] * leaf_one[2]
         return w, act, node, regrets, leaf_one, node_one * kept[w, 3, 0:hands]
 
-    def collect(k, carry):
-        pair = lax.rem(z_self // 2 - far_first(k // 6, 2) + 8, 4)
-        w = 6 * pair + lax.rem(k, 6)
+    def collect(w):
         peer = worker_leaf(w, line)
 
         @pl.when(peer != leaf)
@@ -528,8 +551,6 @@
                 device_id_type=MESH,
             ).wait_recv()
 
-        return carry
-
     def renew(values):
         w, act, node, regrets, leaf_one, node_one = values
         r = rz[pl.ds(w, hands, stride=WORKERS)]
@@ -539,24 +560,37 @@
         for v in range(3):
             new_ro[pl.ds(3 * w + v, hands, stride=3 * WORKERS)] = native[v]
 
+    def trio_values(k, arriving):
+        first = first_of(k)
+        if arriving:
+            for m in range(TRIO):
+                collect(first + m)
+        return [values_of(first + m, m) for m in range(TRIO)]
+
+    def added(carry, trio):
+        sum_zero, sum_one = carry
+        for values in trio:
+            sum_zero = sum_zero + values[2]
+            sum_one = sum_one + values[5]
+        return sum_zero, sum_one
+
     def update(k, carry):
-        collect(k, 0)
-        values = values_of(k)
-        renew(values)
-        return (carry[0] + values[2], carry[1] + values[5])
+        trio = trio_values(k, True)
+        for values in trio:
+            renew(values)
+        return added(carry, trio)
 
     def sum_only(k, carry):
-        collect(k, 0)
-        values = values_of(k)
-        return (carry[0] + values[2], carry[1] + values[5])
+        return added(carry, trio_values(k, True))
 
     def finish(k, carry):
-        renew(values_of(k))
+        for values in trio_values(k, False):
+            renew(values)
         return carry
 
     zero = jnp.zeros((hands, 128), F32)
     sums = lax.fori_loop(0, EARLY, update, (zero, zero))
-    sum_zero, sum_one = lax.fori_loop(EARLY, WORKERS, sum_only, sums)
+    sum_zero, sum_one = lax.fori_loop(EARLY, WORKERS // TRIO, sum_only, sums)
     sum_zero = jnp.where(lane % 64 < SUBGAMES, sum_zero, 0.0)
     values = [
         CHANCE
@@ -572,10 +606,10 @@
     own[0] = turn_share * values[0]
     own[1] = values[1]
     line_start(own, parts, root_send, root_recv)
-    lax.fori_loop(EARLY, WORKERS, finish, 0)
+    lax.fori_loop(EARLY, WORKERS // TRIO, finish, 0)
     stores = [
-        pltpu.make_async_copy(new_rz, rz_out, load_sem.at[2]),
-        pltpu.make_async_copy(new_ro, ro_out, load_sem.at[3]),
+        pltpu.make_async_copy(new_rz, rz_out, store_sem.at[0]),
+        pltpu.make_async_copy(new_ro, ro_out, store_sem.at[1]),
     ]
     for store in stores:
         store.start()
@@ -627,7 +661,6 @@
 
 
 VM = pl.BlockSpec(memory_space=pltpu.VMEM)
-SM = pl.BlockSpec(memory_space=pltpu.SMEM)
 HB = pl.BlockSpec(memory_space=pl.ANY)
 LIMIT = 56 << 20
 
@@ -659,11 +692,19 @@
             jax.ShapeDtypeStruct(ro.shape, F32),
             jax.ShapeDtypeStruct((2,) + tr.shape, F32),
         ),
-        in_specs=[HB, HB, VM, VM, VM, VM, VM, SM, SM, SM],
+        in_specs=[HB] * 10,
         out_specs=(VM, HB, HB, VM),
         scratch_shapes=[
+            pltpu.VMEM(tr.shape, F32),
+            pltpu.VMEM(ro.shape, F32),
+            pltpu.VMEM(tr.shape, F32),
+            pltpu.SMEM(leaf_pots.shape, jnp.int32),
+            pltpu.SMEM(leaf_kinds.shape, jnp.int32),
             pltpu.VMEM(rz.shape, F32),
-            pltpu.VMEM(ro.shape, F32),
+            pltpu.VMEM(tr.shape, F32),
+            pltpu.VMEM((2, PEERS * hands), jnp.int32),
+            pltpu.VMEM(hand_ranks.shape, jnp.int32),
+            pltpu.SMEM(dealt_cards.shape, jnp.int32),
             pltpu.VMEM(rz.shape, F32),
             pltpu.VMEM(ro.shape, F32),
             pltpu.VMEM((lines,) + tr.shape, F32),
@@ -683,7 +724,8 @@
             pltpu.VMEM((WORKERS, ROWS, 128), i16),
             pltpu.VMEM((2,) + tr.shape, F32),
             pltpu.VMEM((lines, 2) + tr.shape, F32),
-            dma((4,)),
+            dma((10,)),
+            dma((2,)),
             dma((lines,)),
             dma((lines,)),
             dma((2, WORKERS)),
@@ -697,16 +739,16 @@
             collective_id=1, has_side_effects=True, vmem_limit_bytes=LIMIT
         ),
     )(
+        tr,
+        ro,
+        range_one,
+        leaf_pots,
+        leaf_kinds,
         rz,
-        ro,
         range_zero,
-        range_one,
-        tr,
         hand_cards.T,
         hand_ranks,
         dealt_cards,
-        leaf_pots,
-        leaf_kinds,
     )
     results = (new_turn, new_rz, new_ro, roots)
     new_turn, new_rz, new_ro, roots = pl.pallas_call(

time: 70.4 us -> 67.1 us (0.953)
  Pallas kernels: 69.3 us -> 65.8 us
    pallas_call x1, Pallas kernels: 66.5 us -> 63.1 us  [local(): pl.pallas_call(kernel, out_shape=(jax.ShapeDtypeStruct(tr.shape, F32), ja...]
where the time goes in v6:
time: 67.1 us; the launch traced here: 66.5 us
  Pallas kernels  65.8 us (98%)
    pallas_call x1, Pallas kernels, local(): pl.pallas_call(kernel, out_shape=(jax.ShapeDtypeStruct(tr.shape, F32), ja...  63.1 us
    pallas_call x1, Pallas kernels, local(): pl.pallas_call(place_kernel, out_shape=tuple((jax.ShapeDtypeStruct(r.shap...  2.79 us

profile of v6, /device:TPU:38, one launch (start us, length us, event | category | flops | bytes accessed | tf_op | source)
XLA Modules:
  0.0 66.5 jit_solution(17104307115626564744)
XLA Ops:
  0.6 63.1 %shard_map.129 = (f32[16,42]{1,0:T(8,128)}, f32[1008,128]{1,0:T(8,128)}, f32[3024,128]{1,0:T(8,128)}, f32[2,16,42]{2,1,0:T(8,128)}) custom-call(f32[16,42]{1,0:T(8,128)} %bitcast.10, f32[3024,128]{1,0:T(8,128)} %bitcast.7, f32[16,42]{1,0:T(8,128)} %range_one_hbm.1, s32[1,12]{1,0:T(1,128)} %pots_hbm.1, s32[1,12]{1,0:T(1,128)} %kinds_hbm.1, ...), custom_call_target="tpu_custom_call" | custom-call | tf_op jit(solution)/shard_map/pallas_call | solution.py:687
  63.7 2.8 %shard_map.130 = (f32[16,42]{1,0:T(8,128)}, f32[1008,128]{1,0:T(8,128)}, f32[3024,128]{1,0:T(8,128)}, f32[2,16,42]{2,1,0:T(8,128)}) custom-call(f32[16,42]{1,0:T(8,128)} %get-tuple-element.12.refs_0_, f32[1008,128]{1,0:T(8,128)} %get-tuple-element.13.refs_1_, f32[3024,128]{1,0:T(8,128)} %get-tuple-element.14.refs_2_, f32[2,16,42]{2,1,0:T(8,128)} %get-tuple-element.15.refs_3_), custom_call_target="tpu_custom_call" | custom-call | tf_op jit(solution)/shard_map/pallas_call | solution.py:754

commit v7 on v6

--- a/solution.py
+++ b/solution.py
@@ -121,6 +121,7 @@
 EARLY = 5
 PLANE = 4
 TRIO = 3
+PIECES = 3
 
 
 def column(rows, select):
@@ -349,17 +350,19 @@
     weight_zero = to_lanes(range_zero[...] * turn_share)
 
     def prepare_zero(k, carry):
-        w = forward_worker(k)
-        _, zs = zero_shares(rz, w, lane, hands)
-        kept[w, 4, 0:hands] = zs
-        z = (weight_zero * zs).astype(BF16).astype(F32)
-        power = power_above(jnp.max(z, axis=0, keepdims=True))
-        y_stage[w, 2 * hands : 3 * hands] = nearest(z * (CODE * jnp.exp2(-power)))
-        y_stage[w, 3 * hands : 3 * hands + 1] = power
-        hand_over(1, w)
+        workers = [forward_worker(TRIO * k + m) for m in range(TRIO)]
+        for w in workers:
+            _, zs = zero_shares(rz, w, lane, hands)
+            kept[w, 4, 0:hands] = zs
+            z = (weight_zero * zs).astype(BF16).astype(F32)
+            power = power_above(jnp.max(z, axis=0, keepdims=True))
+            y_stage[w, 2 * hands : 3 * hands] = nearest(z * (CODE * jnp.exp2(-power)))
+            y_stage[w, 3 * hands : 3 * hands + 1] = power
+        for w in workers:
+            hand_over(1, w)
         return carry
 
-    lax.fori_loop(0, WORKERS, prepare_zero, 0)
+    lax.fori_loop(0, WORKERS // TRIO, prepare_zero, 0)
 
     def out_copy(peer):
         return pltpu.make_async_remote_copy(
@@ -454,7 +457,7 @@
             s_high = jnp.floor(ws * (1.0 / 256.0))
             s_low = ws - 256.0 * s_high
             x[rows, 384:512] = jnp.where(low, s_high, roll_half(s_low)).astype(BF16)
-            x[rows, 512:640] = jnp.where(low, roll_half(s_high), s_low).astype(BF16)
+            x[rows, 640:768] = jnp.where(low, roll_half(s_high), s_low).astype(BF16)
             return w_sum + ws
 
         def arrive_two(k, carry):
@@ -466,9 +469,10 @@
             z = (flat(stage[0:PLANE, 2 * hands : 2 * hands + HP] * scale) * v).astype(BF16)
             f_high = jnp.floor(wf * (1.0 / 256.0))
             f_low = wf - 256.0 * f_high
-            x[rows, 0:128] = z
-            x[rows, 128:256] = f_high.astype(BF16)
-            x[rows, 256:384] = f_low.astype(BF16)
+            x[rows, 0:128] = f_high.astype(BF16)
+            x[rows, 128:256] = f_low.astype(BF16)
+            x[rows, 256:384] = z
+            x[rows, 512:640] = z
             return (z_sum + z.astype(F32), w_sum + jnp.abs(wf))
 
         empty = jnp.zeros((PLANE * HP, 128), F32)
@@ -484,20 +488,20 @@
             i = lax.rem(z_self // 2 + far_first(k, 2), 4)
             rows = pl.ds(pl.multiple_of(i * BLOCK, BLOCK), BLOCK)
             d = jnp.dot(mat[2, rows], x[:, 0:384], preferred_element_type=F32)
-            s0z = jnp.dot(mat[0, rows], x[:, 0:128], preferred_element_type=F32)
-            s0w = jnp.dot(mat[0, rows], x[:, 384:512], preferred_element_type=F32)
-            s1z = jnp.dot(mat[1, rows], x[:, 0:128], preferred_element_type=F32)
-            s1w = jnp.dot(mat[1, rows], x[:, 512:640], preferred_element_type=F32)
+            s0 = jnp.dot(mat[0, rows], x[:, 256:512], preferred_element_type=F32)
+            s1 = jnp.dot(mat[1, rows], x[:, 512:768], preferred_element_type=F32)
+            s0z, s0w = s0[:, 0:128], s0[:, 128:256]
+            s1z, s1w = s1[:, 0:128], s1[:, 128:256]
             v = col[2, rows]
             s0w = s0w * low_part
             s1w = s1w * low_part
             s0w = s0w + roll_half(s0w)
             s1w = s1w + roll_half(s1w)
-            act = jnp.where(low, s0w, s1w) + 256.0 * d[:, 128:256] + d[:, 256:384]
+            act = jnp.where(low, s0w, s1w) + 256.0 * d[:, 0:128] + d[:, 128:256]
             tiles = (
                 act * (v * w_scale),
                 jnp.where(low, s0z, s1z) * (v * z_scale),
-                d[:, 0:128] * (v * z_scale),
+                d[:, 256:384] * (v * z_scale),
             )
             tiles = [nearest(jnp.minimum(jnp.maximum(t, -CODE), CODE)) for t in tiles]
             for m in range(BLOCK // HP):
@@ -648,16 +652,22 @@
     count = (len(refs) - 2) // 3
     srcs, dsts, held = refs[:count], refs[count : 2 * count], refs[2 * count : 3 * count]
     load_sem, store_sem = refs[-2], refs[-1]
-    loads, stores = [], []
+    pieces = []
     for k in range(count):
-        loads.append(pltpu.make_async_copy(srcs[k], held[k], load_sem.at[k]))
-        stores.append(pltpu.make_async_copy(held[k], dsts[k], store_sem.at[k]))
-        loads[k].start()
-    for k in range(count):
-        loads[k].wait()
-        stores[k].start()
-    for k in range(count):
-        stores[k].wait()
+        rows = srcs[k].shape[0]
+        parts = PIECES if rows % (8 * PIECES) == 0 else 1
+        for m in range(parts):
+            piece = pl.ds(m * (rows // parts), rows // parts)
+            pieces.append((srcs[k].at[piece], held[k].at[piece], dsts[k].at[piece]))
+    loads = [pltpu.make_async_copy(p[0], p[1], load_sem.at[n]) for n, p in enumerate(pieces)]
+    stores = [pltpu.make_async_copy(p[1], p[2], store_sem.at[n]) for n, p in enumerate(pieces)]
+    for load in loads:
+        load.start()
+    for load, store in zip(loads, stores):
+        load.wait()
+        store.start()
+    for store in stores:
+        store.wait()
 
 
 VM = pl.BlockSpec(memory_space=pltpu.VMEM)
@@ -716,7 +726,7 @@
             pltpu.VMEM((PEERS * hands, KP), BF16),
             pltpu.VMEM((8, PEERS * hands), F32),
             pltpu.VMEM((8, KP), F32),
-            pltpu.VMEM((KP, 640), BF16),
+            pltpu.VMEM((KP, 768), BF16),
             pltpu.VMEM((3, KP, KP), BF16),
             pltpu.VMEM((3, KP, 128), F32),
             pltpu.VMEM((KP, 128), BF16),
@@ -756,7 +766,7 @@
         out_shape=tuple(jax.ShapeDtypeStruct(r.shape, F32) for r in results),
         in_specs=[HB] * 4,
         out_specs=(HB,) * 4,
-        scratch_shapes=[pltpu.VMEM(r.shape, F32) for r in results] + [dma((4,)), dma((4,))],
+        scratch_shapes=[pltpu.VMEM(r.shape, F32) for r in results] + [dma((4 * PIECES,)), dma((4 * PIECES,))],
     )(*results)
     return (
         new_turn[None],

time: 67.1 us -> 66.4 us (0.990)
  Pallas kernels: 65.8 us -> 65.1 us
where the time goes in v7:
time: 66.4 us; the launch traced here: 65.8 us
  Pallas kernels  65.1 us (98%)
    pallas_call x1, Pallas kernels, local(): pl.pallas_call(kernel, out_shape=(jax.ShapeDtypeStruct(tr.shape, F32), ja...  62.5 us
    pallas_call x1, Pallas kernels, local(): pl.pallas_call(place_kernel, out_shape=tuple((jax.ShapeDtypeStruct(r.shap...  2.65 us

profile of v7, /device:TPU:38, one launch (start us, length us, event | category | flops | bytes accessed | tf_op | source)
XLA Modules:
  0.0 65.8 jit_solution(4585773140907985105)
XLA Ops:
  0.6 62.5 %shard_map.129 = (f32[16,42]{1,0:T(8,128)}, f32[1008,128]{1,0:T(8,128)}, f32[3024,128]{1,0:T(8,128)}, f32[2,16,42]{2,1,0:T(8,128)}) custom-call(f32[16,42]{1,0:T(8,128)} %bitcast.10, f32[3024,128]{1,0:T(8,128)} %bitcast.7, f32[16,42]{1,0:T(8,128)} %range_one_hbm.1, s32[1,12]{1,0:T(1,128)} %pots_hbm.1, s32[1,12]{1,0:T(1,128)} %kinds_hbm.1, ...), custom_call_target="tpu_custom_call" | custom-call | tf_op jit(solution)/shard_map/pallas_call | solution.py:697
  63.1 2.7 %shard_map.130 = (f32[16,42]{1,0:T(8,128)}, f32[1008,128]{1,0:T(8,128)}, f32[3024,128]{1,0:T(8,128)}, f32[2,16,42]{2,1,0:T(8,128)}) custom-call(f32[16,42]{1,0:T(8,128)} %get-tuple-element.12.refs_0_, f32[1008,128]{1,0:T(8,128)} %get-tuple-element.13.refs_1_, f32[3024,128]{1,0:T(8,128)} %get-tuple-element.14.refs_2_, f32[2,16,42]{2,1,0:T(8,128)} %get-tuple-element.15.refs_3_), custom_call_target="tpu_custom_call" | custom-call | tf_op jit(solution)/shard_map/pallas_call | solution.py:764

commit v8 on v7

--- a/solution.py
+++ b/solution.py
@@ -118,7 +118,7 @@
 ROWS = 128
 STAGE = 136
 SPLIT = 80
-EARLY = 5
+EARLY = 4
 PLANE = 4
 TRIO = 3
 PIECES = 3
@@ -277,21 +277,15 @@
         )
 
     def line_start(src, dst, sends, recvs):
-        def start(k, carry):
+        for k in range(1, lines):
             line_copy(src, dst, sends, recvs, lax.rem(line + k, lines), line).start()
-            return carry
-
-        lax.fori_loop(1, lines, start, 0)
 
     def line_sum(src, dst, sends, recvs):
         dst[line] = src[...]
 
-        def wait(k, carry):
+        for k in range(1, lines):
             peer = lax.rem(line + k, lines)
             line_copy(src, dst, sends, recvs, peer, peer).wait_recv()
-            return carry
-
-        lax.fori_loop(1, lines, wait, 0)
         total = dst[0]
         for t in range(1, lines):
             total = total + dst[t]

time: 66.4 us -> 66.4 us (level)
  no operation moved by 1% of the time
where the time goes in v8:
time: 66.4 us; the launch traced here: 65.7 us
  Pallas kernels  65.1 us (98%)
    pallas_call x1, Pallas kernels, local(): pl.pallas_call(kernel, out_shape=(jax.ShapeDtypeStruct(tr.shape, F32), ja...  62.4 us
    pallas_call x1, Pallas kernels, local(): pl.pallas_call(place_kernel, out_shape=tuple((jax.ShapeDtypeStruct(r.shap...  2.65 us

profile of v8, /device:TPU:38, one launch (start us, length us, event | category | flops | bytes accessed | tf_op | source)
XLA Modules:
  0.0 65.7 jit_solution(982656473278280806)
XLA Ops:
  0.6 62.4 %shard_map.129 = (f32[16,42]{1,0:T(8,128)}, f32[1008,128]{1,0:T(8,128)}, f32[3024,128]{1,0:T(8,128)}, f32[2,16,42]{2,1,0:T(8,128)}) custom-call(f32[16,42]{1,0:T(8,128)} %bitcast.10, f32[3024,128]{1,0:T(8,128)} %bitcast.7, f32[16,42]{1,0:T(8,128)} %range_one_hbm.1, s32[1,12]{1,0:T(1,128)} %pots_hbm.1, s32[1,12]{1,0:T(1,128)} %kinds_hbm.1, ...), custom_call_target="tpu_custom_call" | custom-call | tf_op jit(solution)/shard_map/pallas_call | solution.py:691
  63.1 2.7 %shard_map.130 = (f32[16,42]{1,0:T(8,128)}, f32[1008,128]{1,0:T(8,128)}, f32[3024,128]{1,0:T(8,128)}, f32[2,16,42]{2,1,0:T(8,128)}) custom-call(f32[16,42]{1,0:T(8,128)} %get-tuple-element.12.refs_0_, f32[1008,128]{1,0:T(8,128)} %get-tuple-element.13.refs_1_, f32[3024,128]{1,0:T(8,128)} %get-tuple-element.14.refs_2_, f32[2,16,42]{2,1,0:T(8,128)} %get-tuple-element.15.refs_3_), custom_call_target="tpu_custom_call" | custom-call | tf_op jit(solution)/shard_map/pallas_call | solution.py:758
